TPU v7x, 32 devices: a whole 2x2x4 slice. The times are simulated.
32 devices in a mesh: wa: 8 (over z, x), af: 4 (over y, core).
Axes of the slice: x: 2, y: 2, z: 4, core: 2. Of those that a mesh axis runs over, the one named last changes fastest.
Arguments:
- worker_ids: int32 [131072], P(('wa', 'af')), may hold values from 0 to 32767, as said below
- worker_attrs: bfloat16 [131072, 128], P(('wa', 'af')), may hold values from -16 to 16
- firm_ids: int32 [131072], P(('wa', 'af')), may hold values from 0 to 16383, as said below
- firm_attrs: bfloat16 [131072, 128], P(('wa', 'af')), may hold values from -16 to 16
- affinity: bfloat16 [128, 128], replicated, may hold values from -0.5 to 0.5
Outputs:
- worker_means: float32 [32768, 128], P('wa')
- firm_means: float32 [16384, 128], P('af')
- worker_potential: float32 [32768], P('wa')
- firm_potential: float32 [16384], P('af')
Inputs may be any that keep to these rules, and one draw needn't show every extreme that they name: `worker_ids`: type ids come in blocks of 4096 consecutive worker types; in the rows of one device at most 1024 records name one block, and in every device's rows some block is named by exactly 1024. Counts per type are skewed and some types have no record. `firm_ids`: type ids come in blocks of 4096 consecutive firm types; in the rows of one device at most 2048 records name one block, and in every device's rows some block is named by exactly 2048. Counts per type are skewed and some types have no record.
All inputs are finite; a program needn't handle non-finite values.
Results may differ from a plain program's by a relative error of at most 0.00205.
The roundings to bfloat16 on the way count: a program that leaves them out, or rounds other values in their place, can miss the bound.
Values may be sent and summed in bfloat16 or wider, within the bound.
A program may use at most 64 MiB of HBM per device.

v0:
```python
import math

import jax
import jax.numpy as jnp
from jax import lax
from jax.sharding import PartitionSpec as P

W = 32768
F = 16384
ITERS = 3


def joined(value, axis, combine):
    everything = jax.tree.map(lambda part: lax.all_gather(part, axis), value)
    initial = jax.tree.map(lambda part: part[0], everything)

    def step(k, so_far):
        return combine(so_far, jax.tree.map(lambda part: part[k], everything))

    return lax.fori_loop(1, lax.axis_size(axis), step, initial)


def merge_pair(left, right):
    peak = jnp.maximum(left[0], right[0])
    return (peak, left[1] * jnp.exp(left[0] - peak) + right[1] * jnp.exp(right[0] - peak))


def pack_records(type_ids, attrs, tile, groups, capacity):
    owner = type_ids // tile
    local = type_ids - owner * tile
    order = jnp.argsort(owner, stable=True)
    owner_sorted = owner[order]
    matches = (owner_sorted[:, None] == jnp.arange(groups, dtype=jnp.int32)[None, :]).astype(
        jnp.int32
    )
    tallies = jnp.sum(matches, axis=0)
    starts = jnp.cumsum(tallies) - tallies
    slot = jnp.arange(type_ids.shape[0], dtype=jnp.int32) - jnp.sum(
        matches * starts[None, :], axis=1
    )
    place = owner_sorted * capacity + slot
    width = attrs.shape[1]
    sent_attrs = jnp.zeros((groups * capacity, width), attrs.dtype).at[place].set(attrs[order])
    sent_ids = jnp.full((groups * capacity,), tile, jnp.int32).at[place].set(local[order])
    return (sent_attrs.reshape(groups, capacity, width), sent_ids.reshape(groups, capacity))


def pool_records(recv_attrs, recv_ids, tile):
    width = recv_attrs.shape[2]
    flat_ids = recv_ids.reshape(-1)
    totals = jax.ops.segment_sum(
        recv_attrs.reshape(-1, width).astype(jnp.float32), flat_ids, num_segments=tile + 1
    )[:tile]
    tallies = jax.ops.segment_sum(
        jnp.ones(flat_ids.shape, jnp.float32), flat_ids, num_segments=tile + 1
    )[:tile]
    return (totals, tallies)


def body(worker_ids, worker_attrs, firm_ids, firm_attrs, affinity):
    rows = worker_ids.shape[0]
    wa_count = lax.axis_size("wa")
    af_count = lax.axis_size("af")
    worker_tile = W // wa_count
    firm_tile = F // af_count
    records_all = rows * wa_count * af_count
    sent_attrs, sent_ids = pack_records(
        worker_ids, worker_attrs, worker_tile, wa_count, 2 * rows // wa_count
    )
    recv_attrs, recv_ids = (
        lax.all_to_all(sent_attrs, "wa", split_axis=0, concat_axis=0, tiled=True),
        lax.all_to_all(sent_ids, "wa", split_axis=0, concat_axis=0, tiled=True),
    )
    worker_sum, worker_tally = pool_records(recv_attrs, recv_ids, worker_tile)
    sent_attrs, sent_ids = pack_records(
        firm_ids, firm_attrs, firm_tile, af_count, 2 * rows // af_count
    )
    recv_attrs, recv_ids = (
        lax.all_to_all(sent_attrs, "af", split_axis=0, concat_axis=0, tiled=True),
        lax.all_to_all(sent_ids, "af", split_axis=0, concat_axis=0, tiled=True),
    )
    firm_sum, firm_tally = pool_records(recv_attrs, recv_ids, firm_tile)
    worker_sum, worker_tally = lax.psum((worker_sum, worker_tally), "af")
    worker_means = worker_sum / jnp.maximum(worker_tally, 1.0)[:, None]
    firm_sum, firm_tally = lax.psum((firm_sum, firm_tally), "wa")
    firm_means = firm_sum / jnp.maximum(firm_tally, 1.0)[:, None]
    log_worker = jnp.log(worker_tally + 1.0) - jnp.log(jnp.float32(records_all + W))
    log_firm = jnp.log(firm_tally + 1.0) - jnp.log(jnp.float32(records_all + F))
    projected = jnp.dot(
        worker_means.astype(jnp.bfloat16), affinity, preferred_element_type=jnp.float32
    ).astype(jnp.bfloat16)
    firm_rows = firm_means.astype(jnp.bfloat16)
    height = math.gcd(worker_tile, 512)
    blocks = worker_tile // height

    def surplus(index):
        rows_block = lax.dynamic_slice_in_dim(projected, index * height, height, 0)
        return jnp.dot(rows_block, firm_rows.T, preferred_element_type=jnp.float32)

    firm_potential = jnp.zeros((firm_tile,), jnp.float32)
    worker_potential = jnp.zeros((worker_tile,), jnp.float32)
    for rounds in range(ITERS):

        def row_stats(index, shift=firm_potential):
            scores = surplus(index) + shift[None, :]
            peak = jnp.max(scores, axis=1)
            return (peak, jnp.sum(jnp.exp(scores - peak[:, None]), axis=1))

        peak, total = lax.map(row_stats, jnp.arange(blocks, dtype=jnp.int32))
        row_peak = peak.reshape(worker_tile)
        row_total = total.reshape(worker_tile)
        peak, total = joined((row_peak, row_total), "af", merge_pair)
        worker_potential = log_worker - (peak + jnp.log(total))

        def col_step(carry, inputs):
            peak, total = carry
            index, shift_block = inputs
            scores = surplus(index) + shift_block[:, None]
            new_peak = jnp.maximum(peak, jnp.max(scores, axis=0))
            total = total * jnp.exp(peak - new_peak) + jnp.sum(
                jnp.exp(scores - new_peak[None, :]), axis=0
            )
            return ((new_peak, total), None)

        start = (jnp.full((firm_tile,), -1e30, jnp.float32), jnp.zeros((firm_tile,), jnp.float32))
        (peak, total), unused = lax.scan(
            col_step,
            start,
            (jnp.arange(blocks, dtype=jnp.int32), worker_potential.reshape(blocks, height)),
        )
        peak, total = joined((peak, total), "wa", merge_pair)
        firm_potential = log_firm - (peak + jnp.log(total))
    return (worker_means, firm_means, worker_potential, firm_potential)


def solution(mesh):
    placed = (P(("wa", "af")), P(("wa", "af"), None), P(("wa", "af")), P(("wa", "af"), None), P())
    return jax.shard_map(
        body,
        mesh=mesh,
        in_specs=placed,
        out_specs=(P("wa", None), P("af", None), P("wa"), P("af")),
        check_vma=False,
    )
```

profile of v0, /device:TPU:0, one launch (start us, length us, event | category | flops | bytes accessed | tf_op | source)
XLA Modules:
  0.0 1129.6 jit_solution(4271473982780954577)
XLA Ops:
  8.0 5.8 sort.32
  13.8 23.0 %gather_fusion.2 = s32[4096]{0:T(1024)S(1)} fusion(s32[4096]{0:T(1024)S(1)} %get-tuple-element.1306, s32[4096]{0:T(1024)S(1)} %fusion.37), kind=kCustom, calls=%fused_computation.3 | custom fusion | bytes 49152 | tf_op jit(solution)/shard_map/gather | solution.py:32
  37.3 23.0 %gather_fusion.3 = s32[4096]{0:T(1024)S(1)} fusion(s32[4096]{0:T(1024)S(1)} %get-tuple-element.1305, s32[4096]{0:T(1024)S(1)} %fusion.37), kind=kCustom, calls=%fused_computation.4 | custom fusion | bytes 49152 | tf_op jit(solution)/shard_map/gather | solution.py:44
  60.4 16.1 %scatter_custom_fusion.4 = s32[8192]{0:T(1024)} fusion(s32[4096]{0:T(1024)S(1)} %bitcast.193, s32[4096]{0:T(1024)S(1)} %gather_fusion.3, s32[]{:T(128)} %constant.358.clone.1), kind=kCustom, calls=%fused_computation.129 | custom fusion | bytes 32772 | tf_op jit(solution)/shard_map/scatter | solution.py:44
  80.8 5.8 sort.31
  86.6 23.0 %gather_fusion = s32[4096]{0:T(1024)S(1)} fusion(s32[4096]{0:T(1024)S(1)} %get-tuple-element.1308, s32[4096]{0:T(1024)S(1)} %fusion.36), kind=kCustom, calls=%fused_computation | custom fusion | bytes 49152 | tf_op jit(solution)/shard_map/gather | solution.py:32
  110.1 23.0 %gather_fusion.1 = s32[4096]{0:T(1024)S(1)} fusion(s32[4096]{0:T(1024)S(1)} %get-tuple-element.1307, s32[4096]{0:T(1024)S(1)} %fusion.36), kind=kCustom, calls=%fused_computation.1 | custom fusion | bytes 49152 | tf_op jit(solution)/shard_map/gather | solution.py:44
  133.1 16.1 %scatter_custom_fusion = s32[8192]{0:T(1024)} fusion(s32[4096]{0:T(1024)S(1)} %bitcast.195, s32[4096]{0:T(1024)S(1)} %gather_fusion.1, s32[]{:T(128)} %constant.358.clone.1), kind=kCustom, calls=%fused_computation.131 | custom fusion | bytes 32772 | tf_op jit(solution)/shard_map/scatter | solution.py:44
  149.2 6.3 all-to-all-start
  155.5 24.6 %scatter_custom_fusion.5 = bf16[8192,128]{1,0:T(8,128)(2,1)} fusion(s32[4096]{0:T(1024)S(1)} %bitcast.194, bf16[4096,128]{1,0:T(8,128)(2,1)S(1)} %copy-done, s32[4096]{0:T(1024)S(1)} %fusion.37, bf16[]{:T(256)} %constant.366.clone.1), kind=kCustom, calls=%fused_computation.80 | custom fusion | bytes 2097154 | tf_op jit(solution)/shard_map/scatter | solution.py:43
  184.0 38.0 %scatter_custom_fusion.1 = bf16[8192,128]{1,0:T(8,128)(2,1)} fusion(s32[4096]{0:T(1024)S(1)} %bitcast.196, bf16[4096,128]{1,0:T(8,128)(2,1)} %param.30, s32[4096]{0:T(1024)S(1)} %fusion.36, bf16[]{:T(256)} %constant.366.clone.1), kind=kCustom, calls=%fused_computation.82 | custom fusion | bytes 2097664 | tf_op jit(solution)/shard_map/scatter | solution.py:43
  222.0 6.0 all-to-all-start.1
  228.1 51.5 %scatter_custom_fusion.6 = f32[4097,128]{1,0:T(8,128)S(1)} fusion(s32[8192]{0:T(1024)S(1)} %bitcast.189, bf16[8192,128]{1,0:T(8,128)(2,1)} %bitcast.146, f32[]{:T(128)} %constant.357.clone.1), kind=kCustom, calls=%fused_computation.74 | custom fusion | flops 2097152 | bytes 4194820 | tf_op jit(solution)/shard_map/scatter-add | solution.py:51
  281.2 50.1 %scatter_custom_fusion.7 = f32[4097]{0:T(1024)S(1)} fusion(s32[8192]{0:T(1024)S(1)} %bitcast.190, f32[8192]{0:T(1024)S(1)} %broadcast.132, f32[]{:T(128)} %constant.357.clone.1), kind=kCustom, calls=%fused_computation.135 | custom fusion | flops 8192 | bytes 16392 | tf_op jit(solution)/shard_map/scatter-add | solution.py:54
  331.3 35.1 %psum.31 = f32[4096]{0:T(1024)S(1)} all-reduce(f32[4096]{0:T(1024)S(1)} %slice.91), channel_id=1, replica_groups=mesh['wa'=8,'af'=4] {'wa'}, use_global_device_ids=true, to_apply=%region_19.20 | all-reduce | flops 4096 | bytes 32768 | tf_op jit(solution)/shard_map/psum | solution.py:85
  366.4 49.1 %scatter_custom_fusion.3 = f32[4097]{0:T(1024)S(1)} fusion(s32[8192]{0:T(1024)S(1)} %bitcast.191, f32[8192]{0:T(1024)S(1)} %broadcast.132, f32[]{:T(128)} %constant.357.clone.1), kind=kCustom, calls=%fused_computation.137 | custom fusion | flops 8192 | bytes 16392 | tf_op jit(solution)/shard_map/scatter-add | solution.py:54
  415.5 14.3 %psum.29 = f32[4096]{0:T(1024)S(1)} all-reduce(f32[4096]{0:T(1024)S(1)} %slice.89), channel_id=1, replica_groups=mesh['wa'=8,'af'=4] {'af'}, use_global_device_ids=true, to_apply=%region_9.10 | all-reduce | flops 4096 | bytes 32768 | tf_op jit(solution)/shard_map/psum | solution.py:83
  429.8 50.6 %scatter_custom_fusion.2 = f32[4097,128]{1,0:T(8,128)S(1)} fusion(s32[8192]{0:T(1024)S(1)} %bitcast.192, bf16[8192,128]{1,0:T(8,128)(2,1)} %bitcast.51, f32[]{:T(128)} %constant.357.clone.1), kind=kCustom, calls=%fused_computation.76 | custom fusion | flops 2097152 | bytes 4194820 | tf_op jit(solution)/shard_map/scatter-add | solution.py:51
  484.9 48.4 %all-reduce.3.cloned.1.call-done = f32[4096,128]{1,0:T(8,128)} async-done(((f32[4096,128]{1,0:T(8,128)}), f32[4096,128]{1,0:T(8,128)}) %all-reduce.3.cloned.1.call-update) | async-done | bytes 2097168 | tf_op jit(solution)/shard_map/psum | solution.py:83
  537.0 32.5 %while.177 = (s32[]{:T(128)}, f32[8,512]{1,0:T(8,128)S(1)}, f32[8,512]{1,0:T(8,128)S(1)}, s32[8]{0:T(128)S(1)}, bf16[4096,128]{1,0:T(8,128)(2,1)S(1)}, /*index=5...) while((s32[]{:T(128)}, f32[8,512]{1,0:T(8,128)S(1)}, ...), condition=%wide.region_23.24_spmd, body=%wide.region_20.23_spmd.sunk | while | flops 543161344 | bytes 17971372 | solution.py:109
  569.5 5.2 all-gather.6
  574.8 5.2 all-gather.7
  580.5 87.7 %while.186 = (s32[]{:T(128)}, f32[4096]{0:T(1024)S(1)}, f32[4096]{0:T(1024)S(1)}, s32[8]{0:T(128)S(1)}, bf16[4096,128]{1,0:T(8,128)(2,1)S(1)}, /*index=5*/bf16[4...) while((s32[]{:T(128)}, f32[4096]{0:T(1024)S(1)}, ...), condition=%wide.region_29.30_spmd.clone, body=%wide.region_26.29_spmd.clone.sunk | while | flops 547377152 | bytes 18178232 | solution.py:126
  586.4 5.0 exponential_reduce_fusion.15
  597.3 5.0 exponential_reduce_fusion.15
  608.3 5.0 exponential_reduce_fusion.15
  619.2 5.0 exponential_reduce_fusion.15
  630.2 5.0 exponential_reduce_fusion.15
  641.2 5.0 exponential_reduce_fusion.15
  652.1 5.0 exponential_reduce_fusion.15
  663.1 5.0 exponential_reduce_fusion.15
  668.2 30.6 %all-gather = f32[32768]{0:T(1024)S(1)} all-gather(f32[4096]{0:T(1024)S(1)} %get-tuple-element.1033), channel_id=2, replica_groups=mesh['wa'=8,'af'=4] {'wa'}, dimensions={0}, use_global_device_ids=true | all-gather | bytes 147456 | tf_op jit(solution)/shard_map/all_gather | solution.py:14
  698.8 30.7 %all-gather.1 = f32[32768]{0:T(1024)S(1)} all-gather(f32[4096]{0:T(1024)S(1)} %get-tuple-element.1034), channel_id=3, replica_groups=mesh['wa'=8,'af'=4] {'wa'}, dimensions={0}, use_global_device_ids=true | all-gather | bytes 147456 | tf_op jit(solution)/shard_map/all_gather | solution.py:14
  730.2 35.4 %while.180 = (s32[]{:T(128)}, f32[8,512]{1,0:T(8,128)S(1)}, f32[8,512]{1,0:T(8,128)S(1)}, s32[8]{0:T(128)S(1)}, bf16[4096,128]{1,0:T(8,128)(2,1)S(1)}, /*index=5...) while((s32[]{:T(128)}, f32[8,512]{1,0:T(8,128)S(1)}, ...), condition=%wide.region_35.36_spmd, body=%wide.region_32.35_spmd.sunk | while | flops 547355648 | bytes 18004148 | solution.py:109
  765.6 5.2 all-gather.8
  770.9 5.2 all-gather.9
  776.6 87.7 %while.187 = (s32[]{:T(128)}, f32[4096]{0:T(1024)S(1)}, f32[4096]{0:T(1024)S(1)}, s32[8]{0:T(128)S(1)}, bf16[4096,128]{1,0:T(8,128)(2,1)S(1)}, /*index=5*/bf16[4...) while((s32[]{:T(128)}, f32[4096]{0:T(1024)S(1)}, ...), condition=%wide.region_41.42_spmd.clone, body=%wide.region_38.41_spmd.clone.sunk | while | flops 547377152 | bytes 18178232 | solution.py:126
  782.5 5.0 exponential_reduce_fusion.16
  793.4 5.0 exponential_reduce_fusion.16
  804.4 5.0 exponential_reduce_fusion.16
  864.3 30.6 %all-gather.2 = f32[32768]{0:T(1024)S(1)} all-gather(f32[4096]{0:T(1024)S(1)} %get-tuple-element.1041), channel_id=4, replica_groups=mesh['wa'=8,'af'=4] {'wa'}, dimensions={0}, use_global_device_ids=true | all-gather | bytes 147456 | tf_op jit(solution)/shard_map/all_gather | solution.py:14
  894.9 30.5 %all-gather.3 = f32[32768]{0:T(1024)S(1)} all-gather(f32[4096]{0:T(1024)S(1)} %get-tuple-element.1042), channel_id=5, replica_groups=mesh['wa'=8,'af'=4] {'wa'}, dimensions={0}, use_global_device_ids=true | all-gather | bytes 147456 | tf_op jit(solution)/shard_map/all_gather | solution.py:14
  926.1 35.4 %while.183 = (s32[]{:T(128)}, f32[8,512]{1,0:T(8,128)S(1)}, f32[8,512]{1,0:T(8,128)S(1)}, s32[8]{0:T(128)S(1)}, bf16[4096,128]{1,0:T(8,128)(2,1)S(1)}, /*index=5...) while((s32[]{:T(128)}, f32[8,512]{1,0:T(8,128)S(1)}, ...), condition=%wide.region_47.48_spmd, body=%wide.region_44.47_spmd.sunk | while | flops 547355648 | bytes 18004148 | solution.py:109
  961.6 5.2 all-gather.10
  966.9 5.4 all-gather.11
  973.3 86.7 %while.188 = (s32[]{:T(128)}, f32[4096]{0:T(1024)S(1)}, f32[4096]{0:T(1024)S(1)}, s32[8]{0:T(128)S(1)}, bf16[4096,128]{1,0:T(8,128)(2,1)S(1)}, /*index=5*/bf16[4...) while((s32[]{:T(128)}, f32[4096]{0:T(1024)S(1)}, ...), condition=%wide.region_53.54_spmd.clone, body=%wide.region_50.53_spmd.clone.sunk | while | flops 547377152 | bytes 18178232 | solution.py:126
  1060.0 30.7 %all-gather.4 = f32[32768]{0:T(1024)S(1)} all-gather(f32[4096]{0:T(1024)S(1)} %get-tuple-element.1049), channel_id=6, replica_groups=mesh['wa'=8,'af'=4] {'wa'}, dimensions={0}, use_global_device_ids=true | all-gather | bytes 147456 | tf_op jit(solution)/shard_map/all_gather | solution.py:14
  1090.8 30.5 %all-gather.5 = f32[32768]{0:T(1024)S(1)} all-gather(f32[4096]{0:T(1024)S(1)} %get-tuple-element.1050), channel_id=7, replica_groups=mesh['wa'=8,'af'=4] {'wa'}, dimensions={0}, use_global_device_ids=true | all-gather | bytes 147456 | tf_op jit(solution)/shard_map/all_gather | solution.py:14
  (457 shorter events, 301.1 us)
Async XLA Ops:
  7.2 148.4 %copy-start = (bf16[4096,128]{1,0:T(8,128)(2,1)S(1)}, bf16[4096,128]{1,0:T(8,128)(2,1)}, u32[]{:S(2)}) copy-start(bf16[4096,128]{1,0:T(8,128)(2,1)} %param.32) | copy-start | bytes 3145732
  37.3 43.5 %copy-start.8 = (s32[4096]{0:T(1024)S(1)}, s32[4096]{0:T(1024)}, u32[]{:S(2)}) copy-start(s32[4096]{0:T(1024)} %param.29) | copy-start | bytes 49156
  76.5 72.8 %all-to-all-start.2 = ((s32[4,1,2048]{2,1,0:T(1,128)}), s32[4,1,2048]{2,1,0:T(1,128)S(1)}, u32[]{:S(2)}, u32[]{:S(2)}) async-start(s32[4,1,2048]{2,1,0:T(1,128)} %bitcast.35), calls=%async_computation.2 | async-start | bytes 65536 | tf_op jit(solution)/shard_map/all_to_all | solution.py:80
  149.2 30.9 %all-to-all-start = ((s32[8,1,1024]{2,1,0:T(1,128)}), s32[8,1,1024]{2,1,0:T(1,128)S(1)}, u32[]{:S(2)}, u32[]{:S(2)}) async-start(s32[8,1,1024]{2,1,0:T(1,128)} %bitcast.26), calls=%async_computation | async-start | bytes 65536 | tf_op jit(solution)/shard_map/all_to_all | solution.py:72
  180.2 41.8 %all-to-all-start.3 = ((bf16[4,2048,128]{2,1,0:T(8,128)(2,1)}), bf16[4,2048,128]{2,1,0:T(8,128)(2,1)S(1)}, u32[]{:S(2)}, u32[]{:S(2)}) async-start(bf16[4,2048,128]{2,1,0:T(8,128)(2,1)} %bitcast.148), calls=%async_computation.3 | async-start | bytes 4194304 | tf_op jit(solution)/shard_map/all_to_all | solution.py:79
  222.0 6.0 copy-start.2
  222.0 207.8 %all-to-all-start.1 = ((bf16[8,1024,128]{2,1,0:T(8,128)(2,1)}), bf16[8,1024,128]{2,1,0:T(8,128)(2,1)}, u32[]{:S(2)}, u32[]{:S(2)}) async-start(bf16[8,1024,128]{2,1,0:T(8,128)(2,1)} %bitcast.147), calls=%async_computation.1 | async-start | bytes 4194304 | tf_op jit(solution)/shard_map/all_to_all | solution.py:71
  228.0 253.9 %all-reduce.5.cloned.1.call-start = ((), (), s32[]{:S(2)}) async-start(), calls=%async_computation.5 | async-start | bytes 4194304 | tf_op jit(solution)/shard_map/psum | solution.py:85
  281.0 252.2 %all-reduce.3.cloned.1.call-start = ((), (), s32[]{:S(2)}) async-start(), calls=%async_computation.4 | async-start | bytes 4194304 | tf_op jit(solution)/shard_map/psum | solution.py:83
  480.4 56.1 %copy-start.7 = (bf16[128,128]{1,0:T(8,128)(2,1)S(1)}, bf16[128,128]{1,0:T(8,128)(2,1)}, u32[]{:S(2)}) copy-start(bf16[128,128]{1,0:T(8,128)(2,1)} %param.33) | copy-start | bytes 98308
  535.2 1.3 copy-start.3
  926.1 46.6 %copy-start.4 = (f32[4096]{0:T(1024)S(1)}, f32[4096]{0:T(1024)}, u32[]{:S(2)}) copy-start(f32[4096]{0:T(1024)} %custom-call.4) | copy-start | bytes 49156
  926.1 46.6 %copy-start.5 = (f32[4096]{0:T(1024)S(1)}, f32[4096]{0:T(1024)}, u32[]{:S(2)}) copy-start(f32[4096]{0:T(1024)} %custom-call.5) | copy-start | bytes 49156
  972.7 0.6 copy-start.6
  1060.0 62.5 %copy-start.1 = (bf16[4096,128]{1,0:T(8,128)(2,1)S(1)}, bf16[4096,128]{1,0:T(8,128)(2,1)}, u32[]{:S(2)}) copy-start(bf16[4096,128]{1,0:T(8,128)(2,1)} %param.32) | copy-start | bytes 3145732
Sparse Core Ops, SparseCore 0:
  281.2 105.6 all-reduce.4
  482.0 51.1 all-reduce.2
where the time goes:
time: 1140 us; the launch traced here: 1130 us
  other arithmetic  378 us (33%)
  blocking collectives  265 us (23%)
  local copies, waits for them, and re-layouts  228 us (20%)
  matrix products  140 us (12%)
  waiting for transfers between devices  48.4 us (4%)
  loops' own time  35.5 us (3%)
  starting transfers between devices  20.5 us (2%)
  between operations  15 us (1%)
    all_gather x12, blocking collectives, joined(): everything = jax.tree.map(lambda part: lax.all_gather(part, axis), value)  215 us
    dot_general x48, matrix products, surplus(): return jnp.dot(rows_block, firm_rows.T, preferred_element_type=jnp.float32)  140 us
    reduce_sum x24, other arithmetic, col_step(): jnp.sum(jnp.exp(scores - new_peak[None, :]), axis=0)  121 us
    scatter-add x2, other arithmetic, pool_records(): jax.ops.segment_sum(recv_attrs.reshape(-1, width).astype(jnp.float32), fl...  102 us
    scatter-add x2, other arithmetic, pool_records(): jax.ops.segment_sum(jnp.ones(flat_ids.shape, jnp.float32), flat_ids, num_...  99.2 us
    scatter x2, local copies, waits for them, and re-layouts, pack_records(): jnp.zeros((groups * capacity, width), attrs.dtype).at[place]  62.6 us
    psum x1, waiting for transfers between devices, body(): worker_sum, worker_tally = lax.psum((worker_sum, worker_tally), 'af')  48.4 us
    gather x2, local copies, waits for them, and re-layouts, pack_records(): local[order]  46.1 us
  transfers between devices with their start and end apart: 6, of which 1 were waited for; matrix products, arithmetic and copies ran while one was open for 30% of the time, Pallas kernels for 0%

commit v1 on v0

v1 whole, which is shorter than its diff:
```python
import functools
import math

import jax
import jax.numpy as jnp
from jax import lax
from jax.experimental import pallas as pl
from jax.experimental.pallas import tpu as pltpu
from jax.sharding import PartitionSpec as P

W = 32768
F = 16384
ITERS = 3
LANES = 128
VMEM_BYTES = 60 * 1024 * 1024
MESH = pl.DeviceIdType.MESH


def select_kernel(chunk, wide, low_ref, sec_ref, attrs_ref, out_ref, rhs_ref):
    rows, width = attrs_ref.shape
    block = out_ref.shape[1]
    step = pl.program_id(0)

    @pl.when(step == 0)
    def _():
        eye = lax.broadcasted_iota(jnp.int32, (LANES, LANES), 0) == lax.broadcasted_iota(
            jnp.int32, (LANES, LANES), 1
        )

        def fill(c, carry):
            sec_row = jnp.broadcast_to(sec_ref[pl.ds(c, 1), :], (LANES, LANES))
            sec_col = jnp.sum(jnp.where(eye, sec_row, 0.0), axis=1, keepdims=True)
            spot = pl.ds(pl.multiple_of(c * LANES, LANES), LANES)
            part = attrs_ref[spot, :].astype(jnp.float32)
            for s in range(wide):
                rhs_ref[spot, s * width : (s + 1) * width] = jnp.where(
                    sec_col == s, part, 0.0
                ).astype(jnp.bfloat16)
            return carry

        lax.fori_loop(0, rows // LANES, fill, 0)

    target = lax.broadcasted_iota(jnp.int32, (block, chunk), 0) + step * block
    total = jnp.zeros((block, wide * width), jnp.float32)
    for c in range(rows // chunk):
        hit = jnp.where(low_ref[c : c + 1, :] == target, 1.0, 0.0).astype(jnp.bfloat16)
        total = total + jnp.dot(
            hit, rhs_ref[c * chunk : (c + 1) * chunk, :], preferred_element_type=jnp.float32
        )
    for s in range(wide):
        out_ref[s] = total[:, s * width : (s + 1) * width].astype(out_ref.dtype)


def select_sum(ids, attrs, count, dtype):
    rows, width = attrs.shape
    wide = 2
    span = count // wide
    block = math.gcd(span, 256)
    chunk = math.gcd(rows, 512)
    sec = ids // span
    low = (ids - sec * span).reshape(rows // chunk, chunk)
    sec = sec.astype(jnp.float32).reshape(rows // LANES, LANES)
    whole = lambda shape: pl.BlockSpec(shape, lambda i: (0,) * len(shape))
    out = pl.pallas_call(
        functools.partial(select_kernel, chunk, wide),
        grid=(span // block,),
        out_shape=jax.ShapeDtypeStruct((wide, span, width), dtype),
        in_specs=[whole(low.shape), whole(sec.shape), whole(attrs.shape)],
        out_specs=pl.BlockSpec((wide, block, width), lambda i: (0, i, 0)),
        scratch_shapes=[pltpu.VMEM((rows, wide * width), jnp.bfloat16)],
        compiler_params=pltpu.CompilerParams(vmem_limit_bytes=VMEM_BYTES),
        cost_estimate=pl.CostEstimate(
            flops=2 * rows * count * width, bytes_accessed=rows * width * 4, transcendentals=0
        ),
        name="select_sum",
    )(low, sec, attrs)
    return out.reshape(count, width)


def pack_records(type_ids, attrs, tile, groups, capacity):
    rows = type_ids.shape[0]
    owner = type_ids // tile
    local = type_ids - owner * tile
    grid = owner.reshape(rows // LANES, LANES)
    hits = (grid[None] == jnp.arange(groups, dtype=jnp.int32)[:, None, None])
    ramp = jnp.arange(LANES, dtype=jnp.int32)
    upper = (ramp[:, None] <= ramp[None, :]).astype(jnp.bfloat16)
    within = jnp.dot(hits.astype(jnp.bfloat16), upper, preferred_element_type=jnp.float32)
    lines = within[:, :, -1]
    line = jnp.arange(rows // LANES, dtype=jnp.int32)
    before = jnp.sum(
        jnp.where(line[None, :, None] < line[None, None, :], lines[:, :, None], 0.0), axis=1
    )
    rank = jnp.sum(jnp.where(hits, within - 1.0 + before[:, :, None], 0.0), axis=0)
    place = (grid * capacity + rank.astype(jnp.int32)).reshape(rows)
    sent_attrs = select_sum(place, attrs, groups * capacity, jnp.bfloat16)
    high, lowd = local // 64, local % 64
    filled = jnp.full((groups * capacity,), tile, jnp.int32)
    chosen = place_ids(place, jnp.stack([high, lowd, jnp.ones_like(high)]), groups, capacity)
    sent_ids = jnp.where(chosen[2] > 0.5, (chosen[0] * 64.0 + chosen[1]).astype(jnp.int32), filled)
    return (sent_attrs.reshape(groups, capacity, attrs.shape[1]), sent_ids.reshape(groups, capacity))


def place_ids(place, digits, groups, capacity):
    slots = groups * capacity
    high, low = place // LANES, place % LANES
    ahead = (high[None, :] == jnp.arange(slots // LANES, dtype=jnp.int32)[:, None])
    behind = (low[None, :] == jnp.arange(LANES, dtype=jnp.int32)[:, None]).astype(jnp.bfloat16)
    out = []
    for d in range(digits.shape[0]):
        left = jnp.where(ahead, digits[d][None, :].astype(jnp.bfloat16), jnp.bfloat16(0))
        out.append(
            lax.dot_general(left, behind, (((1,), (1,)), ((), ())), preferred_element_type=jnp.float32)
        )
    return jnp.stack(out).reshape(digits.shape[0], slots)


def pool_records(recv_attrs, recv_ids, tile):
    width = recv_attrs.shape[2]
    flat_ids = recv_ids.reshape(-1)
    totals = select_sum(flat_ids, recv_attrs.reshape(-1, width), tile, jnp.float32)
    high, low = flat_ids // LANES, flat_ids % LANES
    ahead = (high[None, :] == jnp.arange(tile // LANES, dtype=jnp.int32)[:, None])
    behind = (low[None, :] == jnp.arange(LANES, dtype=jnp.int32)[:, None])
    tallies = lax.dot_general(
        ahead.astype(jnp.bfloat16),
        behind.astype(jnp.bfloat16),
        (((1,), (1,)), ((), ())),
        preferred_element_type=jnp.float32,
    )
    return (totals, tallies.reshape(tile))


def joined(value, axis, combine):
    everything = jax.tree.map(lambda part: lax.all_gather(part, axis), value)
    initial = jax.tree.map(lambda part: part[0], everything)

    def step(k, so_far):
        return combine(so_far, jax.tree.map(lambda part: part[k], everything))

    return lax.fori_loop(1, lax.axis_size(axis), step, initial)


def merge_pair(left, right):
    peak = jnp.maximum(left[0], right[0])
    return (peak, left[1] * jnp.exp(left[0] - peak) + right[1] * jnp.exp(right[0] - peak))


def log_sweeps(projected, firm_rows, log_worker, log_firm):
    worker_tile, firm_tile = projected.shape[0], firm_rows.shape[0]
    height = math.gcd(worker_tile, 512)
    blocks = worker_tile // height

    def surplus(index):
        rows_block = lax.dynamic_slice_in_dim(projected, index * height, height, 0)
        return jnp.dot(rows_block, firm_rows.T, preferred_element_type=jnp.float32)

    def sweep(rounds, carry):
        firm_potential = carry[1]

        def row_stats(index):
            scores = surplus(index) + firm_potential[None, :]
            peak = jnp.max(scores, axis=1)
            return (peak, jnp.sum(jnp.exp(scores - peak[:, None]), axis=1))

        peak, total = lax.map(row_stats, jnp.arange(blocks, dtype=jnp.int32))
        peak, total = joined((peak.reshape(-1), total.reshape(-1)), "af", merge_pair)
        worker_potential = log_worker - (peak + jnp.log(total))

        def col_step(carry, inputs):
            peak, total = carry
            index, shift_block = inputs
            scores = surplus(index) + shift_block[:, None]
            new_peak = jnp.maximum(peak, jnp.max(scores, axis=0))
            total = total * jnp.exp(peak - new_peak) + jnp.sum(
                jnp.exp(scores - new_peak[None, :]), axis=0
            )
            return ((new_peak, total), None)

        start = (
            jnp.full((firm_tile,), -jnp.inf, jnp.float32),
            jnp.zeros((firm_tile,), jnp.float32),
        )
        (peak, total), _ = lax.scan(
            col_step,
            start,
            (jnp.arange(blocks, dtype=jnp.int32), worker_potential.reshape(blocks, height)),
        )
        peak, total = joined((peak, total), "wa", merge_pair)
        return (worker_potential, log_firm - (peak + jnp.log(total)))

    start = (jnp.zeros((worker_tile,), jnp.float32), jnp.zeros((firm_tile,), jnp.float32))
    return lax.fori_loop(0, ITERS, sweep, start)


TINY = 4e-28
LEAST = 1e-25
MOST = 1e30


def sweep_kernel(
    wa_size, af_size, proj_ref, firm_ref, wmass_ref, fmass_ref,
    wsum_ref, fsum_ref, bad_ref,
    e_ref, v_ref, u_ref, col_ref, msg_w, msg_f, msg_b, in_w, in_f, in_b,
    send_w, recv_w, send_f, recv_f, send_b, recv_b,
):
    wa, af = lax.axis_index("wa"), lax.axis_index("af")
    wt, ft = proj_ref.shape[0], firm_ref.shape[1]
    wr, fr = wt // LANES, ft // LANES

    barrier = pltpu.get_barrier_semaphore()
    for d in range(1, af_size):
        pl.semaphore_signal(
            barrier, inc=1, device_id=(wa, lax.rem(af + d, af_size)), device_id_type=MESH
        )
    for d in range(1, wa_size):
        pl.semaphore_signal(
            barrier, inc=1, device_id=(lax.rem(wa + d, wa_size), af), device_id_type=MESH
        )

    eye = lax.broadcasted_iota(jnp.int32, (LANES, LANES), 0) == lax.broadcasted_iota(
        jnp.int32, (LANES, LANES), 1
    )

    def lay(part):
        column = jnp.sum(part, axis=1, keepdims=True)
        return jnp.sum(jnp.where(eye, column, 0.0), axis=0, keepdims=True)

    def exchange(turn, msg, inbox, send, recv, size, along_af):
        copies = []
        for d in range(1, size):
            if along_af:
                peer = (wa, lax.rem(af + d, size))
            else:
                peer = (lax.rem(wa + d, size), af)
            slot = turn * (size - 1) + d - 1
            copies.append(
                pltpu.make_async_remote_copy(
                    src_ref=msg.at[turn],
                    dst_ref=inbox.at[slot],
                    send_sem=send.at[slot],
                    recv_sem=recv.at[slot],
                    device_id=peer,
                    device_id_type=MESH,
                )
            )
        for copy in copies:
            copy.start()
        for copy in copies:
            copy.wait()

    def ordered(turn, msg, inbox, size, me, rows):
        total = jnp.zeros((rows, LANES), jnp.float32)
        peak = jnp.zeros((8, LANES), jnp.float32)
        for k in range(size):
            d = lax.rem(me - k + size, size)
            slot = turn * (size - 1) + jnp.maximum(d - 1, 0)
            own = (d == 0).astype(jnp.float32) > 0.5
            value = jnp.where(own, msg[turn], inbox[slot])
            total = total + value[:rows]
            peak = jnp.maximum(peak, value[rows:])
        return total, peak

    def fill(b, carry):
        spot = pl.ds(pl.multiple_of(b * 256, 256), 256)
        acc = jnp.zeros((256, LANES), jnp.float32)
        for c in range(ft // 512):
            scores = jnp.dot(
                proj_ref[spot, :],
                firm_ref[:, c * 512 : (c + 1) * 512],
                preferred_element_type=jnp.float32,
            )
            grown = jnp.exp(scores)
            e_ref[spot, c * 512 : (c + 1) * 512] = grown.astype(jnp.bfloat16)
            for k in range(4):
                acc = acc + grown[:, k * LANES : (k + 1) * LANES]
        for k in range(2):
            msg_w[0, pl.ds(b * 2 + k, 1), :] = lay(acc[k * LANES : (k + 1) * LANES])
        return carry

    lax.fori_loop(0, wt // 256, fill, 0)
    pl.semaphore_wait(barrier, af_size + wa_size - 2)

    fault = jnp.zeros((8, LANES), jnp.float32)
    infinite = jnp.full((8, LANES), jnp.inf, jnp.float32)

    def row_pass(turn):
        def block(b, carry):
            spot = pl.ds(pl.multiple_of(b * LANES, LANES), LANES)
            acc = jnp.zeros((LANES, LANES), jnp.float32)
            for c in range(fr):
                acc = acc + e_ref[spot, c * LANES : (c + 1) * LANES].astype(
                    jnp.float32
                ) * v_ref[c : c + 1, :]
            msg_w[turn, pl.ds(b, 1), :] = lay(acc)
            return carry

        lax.fori_loop(0, wr, block, 0)

    def col_pass(turn):
        col_ref[...] = jnp.zeros_like(col_ref)

        def block(b, carry):
            spot = pl.ds(pl.multiple_of(b * LANES, LANES), LANES)
            row = jnp.broadcast_to(u_ref[pl.ds(b, 1), :], (LANES, LANES))
            scale = jnp.broadcast_to(
                jnp.sum(jnp.where(eye, row, 0.0), axis=1, keepdims=True), (LANES, LANES)
            )
            for c in range(fr):
                part = e_ref[spot, c * LANES : (c + 1) * LANES].astype(jnp.float32) * scale
                col_ref[c] += jnp.sum(part.reshape(LANES // 8, 8, LANES), axis=0)
            return carry

        lax.fori_loop(0, wr, block, 0)
        msg_f[turn, :fr, :] = jnp.sum(col_ref[...], axis=1)

    def judge(total, peak):
        least = jnp.min(total)
        most = jnp.max(total)
        good = (least > LEAST) & (most < MOST)
        fine = jnp.where(good, least, -1.0)
        return jnp.where(peak * TINY <= fine, 0.0, 1.0)

    for turn in range(ITERS):
        if turn == 0:
            biggest = jnp.ones((8, LANES), jnp.float32)
        else:
            row_pass(turn)
            biggest = jnp.full((8, LANES), jnp.max(v_ref[...]), jnp.float32)
        msg_w[turn, wr:, :] = jnp.where(fault > 0.5, infinite, biggest)
        exchange(turn, msg_w, in_w, send_w, recv_w, af_size, True)
        total, peak = ordered(turn, msg_w, in_w, af_size, af, wr)
        fault = judge(total, peak)
        u = wmass_ref[...] / total
        u_ref[...] = u
        if turn == ITERS - 1:
            wsum_ref[...] = total
        col_pass(turn)
        least_u = jnp.full((8, LANES), jnp.min(u), jnp.float32)
        spoiled = (fault > 0.5) | (least_u < 1e-35)
        msg_f[turn, fr:, :] = jnp.where(
            spoiled, infinite, jnp.full((8, LANES), jnp.max(u), jnp.float32)
        )
        exchange(turn, msg_f, in_f, send_f, recv_f, wa_size, False)
        total, peak = ordered(turn, msg_f, in_f, wa_size, wa, fr)
        fault = judge(total, peak)
        v_ref[...] = fmass_ref[...] / total
        if turn == ITERS - 1:
            fsum_ref[...] = total
    msg_b[0] = fault
    exchange(0, msg_b, in_b, send_b, recv_b, af_size, True)
    for d in range(1, af_size):
        fault = jnp.maximum(fault, in_b[d - 1])
    bad_ref[...] = fault


def fast_sweeps(projected, firm_rows, worker_mass, firm_mass):
    wa_size, af_size = lax.axis_size("wa"), lax.axis_size("af")
    wt, ft = projected.shape[0], firm_rows.shape[0]
    wr, fr = wt // LANES, ft // LANES
    vmem = pl.BlockSpec(memory_space=pltpu.VMEM)
    f32 = jnp.float32
    return pl.pallas_call(
        functools.partial(sweep_kernel, wa_size, af_size),
        out_shape=(
            jax.ShapeDtypeStruct((wr, LANES), f32),
            jax.ShapeDtypeStruct((fr, LANES), f32),
            jax.ShapeDtypeStruct((8, LANES), f32),
        ),
        in_specs=[vmem] * 4,
        out_specs=(vmem, vmem, vmem),
        scratch_shapes=[
            pltpu.VMEM((wt, ft), jnp.bfloat16),
            pltpu.VMEM((fr, LANES), f32),
            pltpu.VMEM((wr, LANES), f32),
            pltpu.VMEM((fr, 8, LANES), f32),
            pltpu.VMEM((ITERS, wr + 8, LANES), f32),
            pltpu.VMEM((ITERS, fr + 8, LANES), f32),
            pltpu.VMEM((1, 8, LANES), f32),
            pltpu.VMEM((ITERS * (af_size - 1), wr + 8, LANES), f32),
            pltpu.VMEM((ITERS * (wa_size - 1), fr + 8, LANES), f32),
            pltpu.VMEM((af_size - 1, 8, LANES), f32),
            pltpu.SemaphoreType.DMA((ITERS * (af_size - 1),)),
            pltpu.SemaphoreType.DMA((ITERS * (af_size - 1),)),
            pltpu.SemaphoreType.DMA((ITERS * (wa_size - 1),)),
            pltpu.SemaphoreType.DMA((ITERS * (wa_size - 1),)),
            pltpu.SemaphoreType.DMA((af_size - 1,)),
            pltpu.SemaphoreType.DMA((af_size - 1,)),
        ],
        compiler_params=pltpu.CompilerParams(
            collective_id=0, has_side_effects=True, vmem_limit_bytes=VMEM_BYTES
        ),
        name="sweeps",
    )(projected, firm_rows.T, worker_mass.reshape(wr, LANES), firm_mass.reshape(fr, LANES))


def body(worker_ids, worker_attrs, firm_ids, firm_attrs, affinity):
    rows = worker_ids.shape[0]
    wa_count = lax.axis_size("wa")
    af_count = lax.axis_size("af")
    worker_tile = W // wa_count
    firm_tile = F // af_count
    records_all = rows * wa_count * af_count
    sent_attrs, sent_ids = pack_records(
        worker_ids, worker_attrs, worker_tile, wa_count, 2 * rows // wa_count
    )
    recv_attrs = lax.all_to_all(sent_attrs, "wa", split_axis=0, concat_axis=0, tiled=True)
    recv_ids = lax.all_to_all(sent_ids, "wa", split_axis=0, concat_axis=0, tiled=True)
    worker_sum, worker_tally = pool_records(recv_attrs, recv_ids, worker_tile)
    sent_attrs, sent_ids = pack_records(
        firm_ids, firm_attrs, firm_tile, af_count, 2 * rows // af_count
    )
    recv_attrs = lax.all_to_all(sent_attrs, "af", split_axis=0, concat_axis=0, tiled=True)
    recv_ids = lax.all_to_all(sent_ids, "af", split_axis=0, concat_axis=0, tiled=True)
    firm_sum, firm_tally = pool_records(recv_attrs, recv_ids, firm_tile)
    worker_sum, worker_tally = lax.psum((worker_sum, worker_tally), "af")
    worker_means = worker_sum / jnp.maximum(worker_tally, 1.0)[:, None]
    firm_sum, firm_tally = lax.psum((firm_sum, firm_tally), "wa")
    firm_means = firm_sum / jnp.maximum(firm_tally, 1.0)[:, None]
    log_worker = jnp.log(worker_tally + 1.0) - jnp.log(jnp.float32(records_all + W))
    log_firm = jnp.log(firm_tally + 1.0) - jnp.log(jnp.float32(records_all + F))
    projected = jnp.dot(
        worker_means.astype(jnp.bfloat16), affinity, preferred_element_type=jnp.float32
    ).astype(jnp.bfloat16)
    firm_rows = firm_means.astype(jnp.bfloat16)
    worker_total, firm_total, bad = fast_sweeps(
        projected,
        firm_rows,
        (worker_tally + 1.0) / jnp.float32(records_all + W),
        (firm_tally + 1.0) / jnp.float32(records_all + F),
    )
    worker_potential, firm_potential = lax.cond(
        bad[0, 0] > 0.5,
        lambda: log_sweeps(projected, firm_rows, log_worker, log_firm),
        lambda: (
            log_worker - jnp.log(worker_total.reshape(-1)),
            log_firm - jnp.log(firm_total.reshape(-1)),
        ),
    )
    return (worker_means, firm_means, worker_potential, firm_potential)


def solution(mesh):
    placed = (P(("wa", "af")), P(("wa", "af"), None), P(("wa", "af")), P(("wa", "af"), None), P())
    return jax.shard_map(
        body,
        mesh=mesh,
        in_specs=placed,
        out_specs=(P("wa", None), P("af", None), P("wa"), P("af")),
        check_vma=False,
    )
```

time: 1140 us -> 856 us (0.75)
  other arithmetic: 378 us -> 96.2 us
  local copies, waits for them, and re-layouts: 228 us -> 47.2 us
  Pallas kernels: 0 us -> 160 us
  blocking collectives: 265 us -> 296 us
  matrix products: 140 us -> 113 us
  waiting for transfers between devices: 48.4 us -> 71.2 us
    scatter-add x4 -> x0, other arithmetic: 201 us -> none  [the longest x2 102 us: pool_records(): jax.ops.segment_sum(recv_attrs.reshape(-1, width).astype(jnp.float32), fl...]
    pallas_call x0 -> x5, Pallas kernels: none -> 160 us  [the longest x1 89 us: fast_sweeps(): pl.pallas_call(functools.partial(sweep_kernel, wa_size, af_size), out_sha...]
    scatter x4 -> x0, local copies, waits for them, and re-layouts: 94.8 us -> none  [the longest x2 62.6 us: pack_records(): jnp.zeros((groups * capacity, width), attrs.dtype).at[place]]
    gather x4 -> x0, local copies, waits for them, and re-layouts: 92.1 us -> none  [the longest x2 46.1 us: pack_records(): local[order]]
    reduce_sum x24, other arithmetic: 121 us -> 41.1 us  [col_step(): jnp.sum(jnp.exp(scores - new_peak[None, :]), axis=0)]
    psum x1, blocking collectives: 35.1 us -> 70.2 us  [body(): firm_sum, firm_tally = lax.psum((firm_sum, firm_tally), 'wa')]
    dot_general x48, matrix products: 140 us -> 106 us  [surplus(): return jnp.dot(rows_block, firm_rows.T, preferred_element_type=jnp.float32)]
    psum x1, waiting for transfers between devices: 0.02 us -> 12.8 us  [body(): firm_sum, firm_tally = lax.psum((firm_sum, firm_tally), 'wa')]
  transfers between devices with their start and end apart: 6 -> 6, of which waited for: 1 -> 3; matrix products, arithmetic and copies ran while one was open for 30% -> 2% of each run, Pallas kernels for 0% -> 8%
where the time goes in v1:
time: 856 us; the launch traced here: 853 us
  blocking collectives  296 us (35%)
  Pallas kernels  160 us (19%)
  matrix products  113 us (13%)
  other arithmetic  96.2 us (11%)
  waiting for transfers between devices  71.2 us (8%)
  local copies, waits for them, and re-layouts  47.2 us (6%)
  loops' own time  35.1 us (4%)
  starting transfers between devices  20.2 us (2%)
  between operations  14.9 us (2%)
    all_gather x12, blocking collectives, joined(): everything = jax.tree.map(lambda part: lax.all_gather(part, axis), value)  215 us
    dot_general x48, matrix products, surplus(): return jnp.dot(rows_block, firm_rows.T, preferred_element_type=jnp.float32)  106 us
    pallas_call x1, Pallas kernels, fast_sweeps(): pl.pallas_call(functools.partial(sweep_kernel, wa_size, af_size), out_sha...  89 us
    pallas_call x4, Pallas kernels, select_sum(): pl.pallas_call(functools.partial(select_kernel, chunk, wide), grid=(span...  70.6 us
    psum x1, blocking collectives, body(): firm_sum, firm_tally = lax.psum((firm_sum, firm_tally), 'wa')  70.2 us
    psum x1, waiting for transfers between devices, body(): worker_sum, worker_tally = lax.psum((worker_sum, worker_tally), 'af')  50 us
    reduce_sum x24, other arithmetic, col_step(): jnp.sum(jnp.exp(scores - new_peak[None, :]), axis=0)  41.1 us
    reduce_sum x24, other arithmetic, row_stats(): return (peak, jnp.sum(jnp.exp(scores - peak[:, None]), axis=1))  37.7 us
  transfers between devices with their start and end apart: 6, of which 3 were waited for; matrix products, arithmetic and copies ran while one was open for 2% of the time, Pallas kernels for 8%

profile of v1, /device:TPU:0, one launch (start us, length us, event | category | flops | bytes accessed | tf_op | source)
XLA Modules:
  0.0 853.2 jit_solution(17344120415701258665)
XLA Ops:
  12.1 4.3 all-to-all-start.2
  20.5 6.3 all-to-all-start
  26.8 16.7 %select_sum.6 = bf16[2,4096,128]{2,1,0:T(8,128)(2,1)} custom-call(s32[8,512]{1,0:T(8,128)} %reshape.378.low_ref, f32[32,128]{1,0:T(8,128)} %get-tuple-element.650.sec_ref, bf16[4096,128]{1,0:T(8,128)(2,1)} %attrs_ref.3), custom_call_target="tpu_custom_call" | custom-call | flops 8589934592 | bytes 2097152 | tf_op jit(solution)/shard_map/select_sum/pallas_call | solution.py:64
  43.5 3.6 all-to-all-start.3
  47.7 16.7 %select_sum.4 = bf16[2,4096,128]{2,1,0:T(8,128)(2,1)} custom-call(s32[8,512]{1,0:T(8,128)} %reshape.370.low_ref, f32[32,128]{1,0:T(8,128)} %get-tuple-element.652.sec_ref, bf16[4096,128]{1,0:T(8,128)(2,1)} %attrs_ref.2), custom_call_target="tpu_custom_call" | custom-call | flops 8589934592 | bytes 2097152 | tf_op jit(solution)/shard_map/select_sum/pallas_call | solution.py:64
  64.4 8.3 all-to-all-done.3
  74.1 6.0 all-to-all-start.1
  81.5 18.6 %select_sum.7 = f32[2,2048,128]{2,1,0:T(8,128)} custom-call(s32[16,512]{1,0:T(8,128)} %fusion.81.low_ref, f32[64,128]{1,0:T(8,128)} %fusion.83.sec_ref, bf16[8192,128]{1,0:T(8,128)(2,1)} %bitcast.109), custom_call_target="tpu_custom_call" | custom-call | flops 8589934592 | bytes 4194304 | tf_op jit(solution)/shard_map/select_sum/pallas_call | solution.py:64
  100.0 2.9 copy.25
  104.0 70.2 %psum.31 = f32[4096]{0:T(1024)S(1)} all-reduce(f32[4096]{0:T(1024)S(1)} %fusion.27), channel_id=1, replica_groups=mesh['wa'=8,'af'=4] {'wa'}, use_global_device_ids=true, to_apply=%region_7.8 | all-reduce | flops 4096 | bytes 32768 | tf_op jit(solution)/shard_map/psum | solution.py:418
  175.8 11.0 %psum.29 = f32[4096]{0:T(1024)S(1)} all-reduce(f32[4096]{0:T(1024)S(1)} %fusion.28), channel_id=1, replica_groups=mesh['wa'=8,'af'=4] {'af'}, use_global_device_ids=true, to_apply=%region_3.4 | all-reduce | flops 4096 | bytes 32768 | tf_op jit(solution)/shard_map/psum | solution.py:416
  189.4 18.6 %select_sum.5 = f32[2,2048,128]{2,1,0:T(8,128)} custom-call(s32[16,512]{1,0:T(8,128)} %fusion.76.low_ref, f32[64,128]{1,0:T(8,128)} %fusion.78.sec_ref, bf16[8192,128]{1,0:T(8,128)(2,1)} %bitcast.108), custom_call_target="tpu_custom_call" | custom-call | flops 8589934592 | bytes 4194304 | tf_op jit(solution)/shard_map/select_sum/pallas_call | solution.py:64
  208.6 12.8 %all-reduce.5.cloned.1.call-done = f32[4096,128]{0,1:T(8,128)} async-done(((f32[4096,128]{0,1:T(8,128)}), f32[4096,128]{0,1:T(8,128)}) %all-reduce.5.cloned.1.call-update) | async-done | bytes 2097168 | tf_op jit(solution)/shard_map/psum | solution.py:418
  225.1 50.0 %all-reduce.3.cloned.1.call-done = f32[4096,128]{1,0:T(8,128)} async-done(((f32[4096,128]{1,0:T(8,128)}), f32[4096,128]{1,0:T(8,128)}) %all-reduce.3.cloned.1.call-update) | async-done | bytes 2097168 | tf_op jit(solution)/shard_map/psum | solution.py:416
  278.8 89.0 %sweeps.1 = (f32[32,128]{1,0:T(8,128)S(1)}, f32[32,128]{1,0:T(8,128)S(1)}, f32[8,128]{1,0:T(8,128)}) custom-call(bf16[4096,128]{1,0:T(8,128)(2,1)S(1)} %convolution_convert_fusion.proj_ref, bf16[128,4096]{1,0:T(8,128)(2,1)S(1)} %bitcast.103, f32[32,128]{1,0:T(8,128)} %get-tuple-element.672.wmass_ref, f32[32,128]{1,0:T(8,128)} %get-tuple-element.669.fmass_ref), custom_call_target="tpu_custom_call" | custom-call | tf_op jit(solution)/shard_map/sweeps/pallas_call | solution.py:363
  369.7 476.7 %conditional.1 = (f32[4096]{0:T(1024)}, f32[4096]{0:T(1024)}) conditional(s32[]{:T(128)} %bitcast.33, (f32[32,128]{1,0:T(8,128)S(1)}, f32[4096]{0:T(1024)S(1)}, f32[32,128]{1,0:T(8,128)S(1)}, f32[4096]{0:T(1024)S(1)}) %tuple.90, (bf16[4096,128]{1,0:T(8,128)(2,1)}, bf16[4096,128]{0,1:T(8,128)(2,1)S(1)}, f32[4096]{0:T(1024)S(1)}, ...), branch_computations={%region_8.9_spmd, %region_9.24_spmd} | conditional | flops 1094802432 | bytes 40246696 | solution.py:432
  370.6 475.8 %while.123 = (s32[]{:T(128)}, f32[4096]{0:T(1024)}, f32[4096]{0:T(1024)}, bf16[4096,128]{1,0:T(8,128)(2,1)}, bf16[4096,128]{1,0:T(8,128)(2,1)S(1)}, /*index=5*/f...) while((s32[]{:T(128)}, f32[4096]{0:T(1024)}, ...), condition=%wide.region_23.23_spmd.clone, body=%wide.region_10.22_spmd.clone.sunk | while | flops 1094802432 | bytes 38149336 | solution.py:193
  370.7 41.7 %while.124 = (s32[]{:T(128)}, f32[8,512]{1,0:T(8,128)S(1)}, f32[8,512]{1,0:T(8,128)S(1)}, s32[8]{0:T(128)S(1)}, bf16[4096,128]{1,0:T(8,128)(2,1)}, /*index=5*/bf...) while((s32[]{:T(128)}, f32[8,512]{1,0:T(8,128)S(1)}, ...), condition=%wide.region_14.13_spmd, body=%wide.region_11.12_spmd.sunk | while | flops 547355648 | bytes 18004156 | solution.py:166
  377.1 2.2 add_reduce_fusion.4
  382.4 2.2 add_reduce_fusion.4
  392.8 2.2 add_reduce_fusion.4
  403.2 2.2 add_reduce_fusion.4
  408.4 2.2 add_reduce_fusion.4
  412.4 5.2 all-gather.12
  417.7 5.2 all-gather.13
  424.6 41.9 %while.126 = (s32[]{:T(128)}, f32[4096]{0:T(1024)S(1)}, f32[4096]{0:T(1024)S(1)}, s32[8]{0:T(128)S(1)}, bf16[4096,128]{1,0:T(8,128)(2,1)}, /*index=5*/bf16[4096,...) while((s32[]{:T(128)}, f32[4096]{0:T(1024)S(1)}, ...), condition=%wide.region_20.19_spmd.clone, body=%wide.region_17.18_spmd.clone.sunk | while | flops 547377152 | bytes 18178240 | solution.py:184
  466.5 30.5 %all-gather.15 = f32[32768]{0:T(1024)S(1)} all-gather(f32[4096]{0:T(1024)S(1)} %get-tuple-element.924), channel_id=3, replica_groups=mesh['wa'=8,'af'=4] {'wa'}, dimensions={0}, use_global_device_ids=true | all-gather | bytes 147456 | tf_op jit(solution)/shard_map/cond/branch_1_fun/while/body/eval_jaxpr/all_gather | solution.py:135
  497.0 30.5 %all-gather.14 = f32[32768]{0:T(1024)S(1)} all-gather(f32[4096]{0:T(1024)S(1)} %get-tuple-element.923), channel_id=2, replica_groups=mesh['wa'=8,'af'=4] {'wa'}, dimensions={0}, use_global_device_ids=true | all-gather | bytes 147456 | tf_op jit(solution)/shard_map/cond/branch_1_fun/while/body/eval_jaxpr/all_gather | solution.py:135
  529.5 41.7 %while.124 = (s32[]{:T(128)}, f32[8,512]{1,0:T(8,128)S(1)}, f32[8,512]{1,0:T(8,128)S(1)}, s32[8]{0:T(128)S(1)}, bf16[4096,128]{1,0:T(8,128)(2,1)}, /*index=5*/bf...) while((s32[]{:T(128)}, f32[8,512]{1,0:T(8,128)S(1)}, ...), condition=%wide.region_14.13_spmd, body=%wide.region_11.12_spmd.sunk | while | flops 547355648 | bytes 18004156 | solution.py:166
  530.7 2.2 add_reduce_fusion.4
  541.2 2.2 add_reduce_fusion.4
  551.6 2.2 add_reduce_fusion.4
  567.2 2.2 add_reduce_fusion.4
  571.2 5.2 all-gather.12
  576.5 5.2 all-gather.13
  583.4 41.8 %while.126 = (s32[]{:T(128)}, f32[4096]{0:T(1024)S(1)}, f32[4096]{0:T(1024)S(1)}, s32[8]{0:T(128)S(1)}, bf16[4096,128]{1,0:T(8,128)(2,1)}, /*index=5*/bf16[4096,...) while((s32[]{:T(128)}, f32[4096]{0:T(1024)S(1)}, ...), condition=%wide.region_20.19_spmd.clone, body=%wide.region_17.18_spmd.clone.sunk | while | flops 547377152 | bytes 18178240 | solution.py:184
  625.3 30.5 %all-gather.15 = f32[32768]{0:T(1024)S(1)} all-gather(f32[4096]{0:T(1024)S(1)} %get-tuple-element.924), channel_id=3, replica_groups=mesh['wa'=8,'af'=4] {'wa'}, dimensions={0}, use_global_device_ids=true | all-gather | bytes 147456 | tf_op jit(solution)/shard_map/cond/branch_1_fun/while/body/eval_jaxpr/all_gather | solution.py:135
  655.8 30.5 %all-gather.14 = f32[32768]{0:T(1024)S(1)} all-gather(f32[4096]{0:T(1024)S(1)} %get-tuple-element.923), channel_id=2, replica_groups=mesh['wa'=8,'af'=4] {'wa'}, dimensions={0}, use_global_device_ids=true | all-gather | bytes 147456 | tf_op jit(solution)/shard_map/cond/branch_1_fun/while/body/eval_jaxpr/all_gather | solution.py:135
  688.3 41.7 %while.124 = (s32[]{:T(128)}, f32[8,512]{1,0:T(8,128)S(1)}, f32[8,512]{1,0:T(8,128)S(1)}, s32[8]{0:T(128)S(1)}, bf16[4096,128]{1,0:T(8,128)(2,1)}, /*index=5*/bf...) while((s32[]{:T(128)}, f32[8,512]{1,0:T(8,128)S(1)}, ...), condition=%wide.region_14.13_spmd, body=%wide.region_11.12_spmd.sunk | while | flops 547355648 | bytes 18004156 | solution.py:166
  689.5 2.2 add_reduce_fusion.4
  700.0 2.2 add_reduce_fusion.4
  715.6 2.2 add_reduce_fusion.4
  726.0 2.2 add_reduce_fusion.4
  730.0 5.2 all-gather.12
  735.3 5.2 all-gather.13
  742.2 41.9 %while.126 = (s32[]{:T(128)}, f32[4096]{0:T(1024)S(1)}, f32[4096]{0:T(1024)S(1)}, s32[8]{0:T(128)S(1)}, bf16[4096,128]{1,0:T(8,128)(2,1)}, /*index=5*/bf16[4096,...) while((s32[]{:T(128)}, f32[4096]{0:T(1024)S(1)}, ...), condition=%wide.region_20.19_spmd.clone, body=%wide.region_17.18_spmd.clone.sunk | while | flops 547377152 | bytes 18178240 | solution.py:184
  784.1 30.5 %all-gather.15 = f32[32768]{0:T(1024)S(1)} all-gather(f32[4096]{0:T(1024)S(1)} %get-tuple-element.924), channel_id=3, replica_groups=mesh['wa'=8,'af'=4] {'wa'}, dimensions={0}, use_global_device_ids=true | all-gather | bytes 147456 | tf_op jit(solution)/shard_map/cond/branch_1_fun/while/body/eval_jaxpr/all_gather | solution.py:135
  814.6 30.5 %all-gather.14 = f32[32768]{0:T(1024)S(1)} all-gather(f32[4096]{0:T(1024)S(1)} %get-tuple-element.923), channel_id=2, replica_groups=mesh['wa'=8,'af'=4] {'wa'}, dimensions={0}, use_global_device_ids=true | all-gather | bytes 147456 | tf_op jit(solution)/shard_map/cond/branch_1_fun/while/body/eval_jaxpr/all_gather | solution.py:135
  (465 shorter events, 226.9 us)
Async XLA Ops:
  7.2 271.2 %copy-start = (bf16[128,128]{1,0:T(8,128)(2,1)S(1)}, bf16[128,128]{1,0:T(8,128)(2,1)}, u32[]{:S(2)}) copy-start(bf16[128,128]{1,0:T(8,128)(2,1)} %param.21) | copy-start | bytes 98308
  9.8 6.5 copy-start.5
  12.1 8.4 all-to-all-start.2
  20.5 23.0 %all-to-all-start = ((s32[8,1,1024]{2,1,0:T(1,128)}), s32[8,1,1024]{2,1,0:T(1,128)S(1)}, u32[]{:S(2)}, u32[]{:S(2)}) async-start(s32[8,1,1024]{2,1,0:T(1,128)} %bitcast.12), calls=%async_computation | async-start | bytes 65536 | tf_op jit(solution)/shard_map/all_to_all | solution.py:408
  43.5 29.3 %all-to-all-start.3 = ((bf16[4,2048,128]{2,1,0:T(8,128)(2,1)}), bf16[4,2048,128]{2,1,0:T(8,128)(2,1)S(1)}, u32[]{:S(2)}, u32[]{:S(2)}) async-start(bf16[4,2048,128]{2,1,0:T(8,128)(2,1)} %bitcast.111), calls=%async_computation.3 | async-start | bytes 4194304 | tf_op jit(solution)/shard_map/all_to_all | solution.py:413
  72.7 1.3 copy-start.4
  74.1 114.0 %all-to-all-start.1 = ((bf16[8,1024,128]{2,1,0:T(8,128)(2,1)}), bf16[8,1024,128]{2,1,0:T(8,128)(2,1)S(1)}, u32[]{:S(2)}, u32[]{:S(2)}) async-start(bf16[8,1024,128]{2,1,0:T(8,128)(2,1)} %bitcast.107), calls=%async_computation.1 | async-start | bytes 4194304 | tf_op jit(solution)/shard_map/all_to_all | solution.py:407
  80.0 141.4 %all-reduce.5.cloned.1.call-start = ((), (), s32[]{:S(2)}) async-start(), calls=%async_computation.5 | async-start | bytes 4194304 | tf_op jit(solution)/shard_map/psum | solution.py:418
  103.0 172.1 %all-reduce.3.cloned.1.call-start = ((), (), s32[]{:S(2)}) async-start(), calls=%async_computation.4 | async-start | bytes 4194304 | tf_op jit(solution)/shard_map/psum | solution.py:416
  188.0 1.3 copy-start.3
  277.1 1.3 copy-start.2
  278.8 90.9 %copy-start.1 = (bf16[4096,128]{1,0:T(8,128)(2,1)}, bf16[4096,128]{1,0:T(8,128)(2,1)S(1)}, u32[]{:S(2)}) copy-start(bf16[4096,128]{1,0:T(8,128)(2,1)S(1)} %convolution_convert_fusion.proj_ref) | copy-start | bytes 3145732
Sparse Core Ops, SparseCore 0:
  103.1 118.2 all-reduce.4
  224.3 50.7 all-reduce.2

commit v2 on v1

--- a/solution.py
+++ b/solution.py
@@ -131,6 +131,13 @@
     return (totals, tallies.reshape(tile))
 
 
+def shared_means(sums, tally, axis):
+    tile, width = sums.shape
+    both = lax.psum(jnp.concatenate([sums, tally.reshape(tile // width, width)], axis=0), axis)
+    tally = both[tile:].reshape(tile)
+    return (both[:tile] / jnp.maximum(tally, 1.0)[:, None], tally)
+
+
 def joined(value, axis, combine):
     everything = jax.tree.map(lambda part: lax.all_gather(part, axis), value)
     initial = jax.tree.map(lambda part: part[0], everything)
@@ -201,8 +208,8 @@
 def sweep_kernel(
     wa_size, af_size, proj_ref, firm_ref, wmass_ref, fmass_ref,
     wsum_ref, fsum_ref, bad_ref,
-    e_ref, v_ref, u_ref, col_ref, msg_w, msg_f, msg_b, in_w, in_f, in_b,
-    send_w, recv_w, send_f, recv_f, send_b, recv_b,
+    e_ref, s_ref, v_ref, u_ref, col_ref, msg_w, msg_f, msg_b, msg_m, in_w, in_f, in_b, in_m,
+    send_w, recv_w, send_f, recv_f, send_b, recv_b, send_m, recv_m,
 ):
     wa, af = lax.axis_index("wa"), lax.axis_index("af")
     wt, ft = proj_ref.shape[0], firm_ref.shape[1]
@@ -222,8 +229,7 @@
         jnp.int32, (LANES, LANES), 1
     )
 
-    def lay(part):
-        column = jnp.sum(part, axis=1, keepdims=True)
+    def lay(column):
         return jnp.sum(jnp.where(eye, column, 0.0), axis=0, keepdims=True)
 
     def exchange(turn, msg, inbox, send, recv, size, along_af):
@@ -246,36 +252,53 @@
             )
         for copy in copies:
             copy.start()
+        return copies
+
+    def finish(copies):
         for copy in copies:
             copy.wait()
 
-    def ordered(turn, msg, inbox, size, me, rows):
+    def arrival(turn, msg, inbox, size, me, k):
+        d = lax.rem(me - k + size, size)
+        slot = turn * (size - 1) + jnp.maximum(d - 1, 0)
+        return jnp.where(d == 0, msg[turn], inbox[slot])
+
+    def ordered(turn, msg, inbox, size, me, rows, weights=None):
         total = jnp.zeros((rows, LANES), jnp.float32)
         peak = jnp.zeros((8, LANES), jnp.float32)
         for k in range(size):
-            d = lax.rem(me - k + size, size)
-            slot = turn * (size - 1) + jnp.maximum(d - 1, 0)
-            own = (d == 0).astype(jnp.float32) > 0.5
-            value = jnp.where(own, msg[turn], inbox[slot])
-            total = total + value[:rows]
+            value = arrival(turn, msg, inbox, size, me, k)
+            part = value[:rows]
+            if weights is not None:
+                part = part * weights[k]
+            total = total + part
             peak = jnp.maximum(peak, value[rows:])
         return total, peak
 
     def fill(b, carry):
         spot = pl.ds(pl.multiple_of(b * 256, 256), 256)
-        acc = jnp.zeros((256, LANES), jnp.float32)
+        peak = jnp.full((256, LANES), -jnp.inf, jnp.float32)
         for c in range(ft // 512):
             scores = jnp.dot(
                 proj_ref[spot, :],
                 firm_ref[:, c * 512 : (c + 1) * 512],
                 preferred_element_type=jnp.float32,
             )
-            grown = jnp.exp(scores)
-            e_ref[spot, c * 512 : (c + 1) * 512] = grown.astype(jnp.bfloat16)
+            s_ref[:, c * 512 : (c + 1) * 512] = scores
             for k in range(4):
-                acc = acc + grown[:, k * LANES : (k + 1) * LANES]
+                peak = jnp.maximum(peak, scores[:, k * LANES : (k + 1) * LANES])
+        peak = jnp.max(peak, axis=1, keepdims=True)
+        shift = jnp.broadcast_to(peak, (256, LANES))
+        acc = jnp.zeros((256, LANES), jnp.float32)
+        for c in range(fr):
+            grown = jnp.exp(s_ref[:, c * LANES : (c + 1) * LANES] - shift)
+            e_ref[spot, c * LANES : (c + 1) * LANES] = grown.astype(jnp.bfloat16)
+            acc = acc + grown
+        total = jnp.sum(acc, axis=1, keepdims=True)
         for k in range(2):
-            msg_w[0, pl.ds(b * 2 + k, 1), :] = lay(acc[k * LANES : (k + 1) * LANES])
+            part = slice(k * LANES, (k + 1) * LANES)
+            msg_w[0, pl.ds(b * 2 + k, 1), :] = lay(total[part])
+            msg_m[0, pl.ds(b * 2 + k, 1), :] = lay(peak[part])
         return carry
 
     lax.fori_loop(0, wt // 256, fill, 0)
@@ -284,7 +307,7 @@
     fault = jnp.zeros((8, LANES), jnp.float32)
     infinite = jnp.full((8, LANES), jnp.inf, jnp.float32)
 
-    def row_pass(turn):
+    def row_pass(turn, scale):
         def block(b, carry):
             spot = pl.ds(pl.multiple_of(b * LANES, LANES), LANES)
             acc = jnp.zeros((LANES, LANES), jnp.float32)
@@ -292,10 +315,11 @@
                 acc = acc + e_ref[spot, c * LANES : (c + 1) * LANES].astype(
                     jnp.float32
                 ) * v_ref[c : c + 1, :]
-            msg_w[turn, pl.ds(b, 1), :] = lay(acc)
+            msg_w[turn, pl.ds(b, 1), :] = lay(jnp.sum(acc, axis=1, keepdims=True))
             return carry
 
         lax.fori_loop(0, wr, block, 0)
+        msg_w[turn, :wr, :] = msg_w[turn, :wr, :] * scale
 
     def col_pass(turn):
         col_ref[...] = jnp.zeros_like(col_ref)
@@ -325,30 +349,38 @@
         if turn == 0:
             biggest = jnp.ones((8, LANES), jnp.float32)
         else:
-            row_pass(turn)
+            row_pass(turn, scale)
             biggest = jnp.full((8, LANES), jnp.max(v_ref[...]), jnp.float32)
         msg_w[turn, wr:, :] = jnp.where(fault > 0.5, infinite, biggest)
-        exchange(turn, msg_w, in_w, send_w, recv_w, af_size, True)
-        total, peak = ordered(turn, msg_w, in_w, af_size, af, wr)
+        copies = exchange(turn, msg_w, in_w, send_w, recv_w, af_size, True)
+        weights = None
+        if turn == 0:
+            finish(exchange(0, msg_m, in_m, send_m, recv_m, af_size, True))
+            peaks = [arrival(0, msg_m, in_m, af_size, af, k) for k in range(af_size)]
+            top = functools.reduce(jnp.maximum, peaks)
+            weights = [jnp.exp(p - top) for p in peaks]
+            scale = jnp.exp(msg_m[0] - top)
+        finish(copies)
+        total, peak = ordered(turn, msg_w, in_w, af_size, af, wr, weights)
         fault = judge(total, peak)
         u = wmass_ref[...] / total
-        u_ref[...] = u
+        u_ref[...] = u * scale
         if turn == ITERS - 1:
-            wsum_ref[...] = total
+            wsum_ref[...] = jnp.log(total) + top
         col_pass(turn)
         least_u = jnp.full((8, LANES), jnp.min(u), jnp.float32)
         spoiled = (fault > 0.5) | (least_u < 1e-35)
         msg_f[turn, fr:, :] = jnp.where(
             spoiled, infinite, jnp.full((8, LANES), jnp.max(u), jnp.float32)
         )
-        exchange(turn, msg_f, in_f, send_f, recv_f, wa_size, False)
+        finish(exchange(turn, msg_f, in_f, send_f, recv_f, wa_size, False))
         total, peak = ordered(turn, msg_f, in_f, wa_size, wa, fr)
         fault = judge(total, peak)
         v_ref[...] = fmass_ref[...] / total
         if turn == ITERS - 1:
-            fsum_ref[...] = total
+            fsum_ref[...] = jnp.log(total)
     msg_b[0] = fault
-    exchange(0, msg_b, in_b, send_b, recv_b, af_size, True)
+    finish(exchange(0, msg_b, in_b, send_b, recv_b, af_size, True))
     for d in range(1, af_size):
         fault = jnp.maximum(fault, in_b[d - 1])
     bad_ref[...] = fault
@@ -371,19 +403,24 @@
         out_specs=(vmem, vmem, vmem),
         scratch_shapes=[
             pltpu.VMEM((wt, ft), jnp.bfloat16),
+            pltpu.VMEM((256, ft), f32),
             pltpu.VMEM((fr, LANES), f32),
             pltpu.VMEM((wr, LANES), f32),
             pltpu.VMEM((fr, 8, LANES), f32),
             pltpu.VMEM((ITERS, wr + 8, LANES), f32),
             pltpu.VMEM((ITERS, fr + 8, LANES), f32),
             pltpu.VMEM((1, 8, LANES), f32),
+            pltpu.VMEM((1, wr, LANES), f32),
             pltpu.VMEM((ITERS * (af_size - 1), wr + 8, LANES), f32),
             pltpu.VMEM((ITERS * (wa_size - 1), fr + 8, LANES), f32),
             pltpu.VMEM((af_size - 1, 8, LANES), f32),
+            pltpu.VMEM((af_size - 1, wr, LANES), f32),
             pltpu.SemaphoreType.DMA((ITERS * (af_size - 1),)),
             pltpu.SemaphoreType.DMA((ITERS * (af_size - 1),)),
             pltpu.SemaphoreType.DMA((ITERS * (wa_size - 1),)),
             pltpu.SemaphoreType.DMA((ITERS * (wa_size - 1),)),
+            pltpu.SemaphoreType.DMA((af_size - 1,)),
+            pltpu.SemaphoreType.DMA((af_size - 1,)),
             pltpu.SemaphoreType.DMA((af_size - 1,)),
             pltpu.SemaphoreType.DMA((af_size - 1,)),
         ],
@@ -413,10 +450,8 @@
     recv_attrs = lax.all_to_all(sent_attrs, "af", split_axis=0, concat_axis=0, tiled=True)
     recv_ids = lax.all_to_all(sent_ids, "af", split_axis=0, concat_axis=0, tiled=True)
     firm_sum, firm_tally = pool_records(recv_attrs, recv_ids, firm_tile)
-    worker_sum, worker_tally = lax.psum((worker_sum, worker_tally), "af")
-    worker_means = worker_sum / jnp.maximum(worker_tally, 1.0)[:, None]
-    firm_sum, firm_tally = lax.psum((firm_sum, firm_tally), "wa")
-    firm_means = firm_sum / jnp.maximum(firm_tally, 1.0)[:, None]
+    worker_means, worker_tally = shared_means(worker_sum, worker_tally, "af")
+    firm_means, firm_tally = shared_means(firm_sum, firm_tally, "wa")
     log_worker = jnp.log(worker_tally + 1.0) - jnp.log(jnp.float32(records_all + W))
     log_firm = jnp.log(firm_tally + 1.0) - jnp.log(jnp.float32(records_all + F))
     projected = jnp.dot(
@@ -433,11 +468,16 @@
         bad[0, 0] > 0.5,
         lambda: log_sweeps(projected, firm_rows, log_worker, log_firm),
         lambda: (
-            log_worker - jnp.log(worker_total.reshape(-1)),
-            log_firm - jnp.log(firm_total.reshape(-1)),
+            log_worker - worker_total.reshape(-1),
+            log_firm - firm_total.reshape(-1),
         ),
     )
-    return (worker_means, firm_means, worker_potential, firm_potential)
+    return (
+        worker_means,
+        firm_means,
+        worker_potential,
+        firm_potential,
+    )
 
 
 def solution(mesh):

time: 856 us -> 391 us (0.46)
  blocking collectives: 296 us -> 0 us
  matrix products: 113 us -> 6.9 us
  waiting for transfers between devices: 71.2 us -> 148 us
  other arithmetic: 96.2 us -> 20.3 us
  local copies, waits for them, and re-layouts: 47.2 us -> 7.67 us
  loops' own time: 35.1 us -> 0.01 us
  Pallas kernels: 160 us -> 172 us
    all_gather x12 -> x0, blocking collectives: 215 us -> none  [joined(): everything = jax.tree.map(lambda part: lax.all_gather(part, axis), value)]
    dot_general x48 -> x0, matrix products: 106 us -> none  [surplus(): return jnp.dot(rows_block, firm_rows.T, preferred_element_type=jnp.float32)]
    psum x2 -> x0, blocking collectives: 81.2 us -> none  [the longest x1 70.2 us: body(): firm_sum, firm_tally = lax.psum((firm_sum, firm_tally), 'wa')]
    reduce_sum x48 -> x0, other arithmetic: 78.8 us -> none  [the longest x24 41.1 us: col_step(): jnp.sum(jnp.exp(scores - new_peak[None, :]), axis=0)]
    all_to_all x1, waiting for transfers between devices: 0.01 us -> 44.1 us  [body(): lax.all_to_all(sent_attrs, 'wa', split_axis=0, concat_axis=0, tiled=True)]
    another operation x13 -> x0, loops' own time: 34.8 us -> none  [the longest x3 17.2 us: sweep(): lax.scan(col_step, start, (jnp.arange(blocks, dtype=jnp.int32), worker_po...]
    psum x2, waiting for transfers between devices: 62.8 us -> 95.7 us  [shared_means(): lax.psum(jnp.concatenate([sums, tally.reshape(tile // width, width)], axi...]
    dynamic_slice x102 -> x0, local copies, waits for them, and re-layouts: 29.3 us -> none  [the longest x48 28.2 us: sweep(): peak, total = lax.map(row_stats, jnp.arange(blocks, dtype=jnp.int32))]
  transfers between devices with their start and end apart: 6 -> 6, of which waited for: 3 -> 4; matrix products, arithmetic and copies ran while one was open for 2% -> 5% of each run, Pallas kernels for 8% -> 18%
where the time goes in v2:
time: 391 us; the launch traced here: 390 us
  Pallas kernels  172 us (44%)
  waiting for transfers between devices  148 us (38%)
  starting transfers between devices  20.4 us (5%)
  other arithmetic  20.3 us (5%)
  between operations  14.9 us (4%)
  local copies, waits for them, and re-layouts  7.67 us (2%)
  matrix products  6.9 us (2%)
    pallas_call x1, Pallas kernels, fast_sweeps(): pl.pallas_call(functools.partial(sweep_kernel, wa_size, af_size), out_sha...  101 us
    psum x2, waiting for transfers between devices, shared_means(): lax.psum(jnp.concatenate([sums, tally.reshape(tile // width, width)], axi...  95.7 us
    pallas_call x4, Pallas kernels, select_sum(): pl.pallas_call(functools.partial(select_kernel, chunk, wide), grid=(span...  70.6 us
    all_to_all x1, waiting for transfers between devices, body(): lax.all_to_all(sent_attrs, 'wa', split_axis=0, concat_axis=0, tiled=True)  44.1 us
    all_to_all x1, waiting for transfers between devices, body(): lax.all_to_all(sent_attrs, 'af', split_axis=0, concat_axis=0, tiled=True)  8.31 us
  transfers between devices with their start and end apart: 6, of which 4 were waited for; matrix products, arithmetic and copies ran while one was open for 5% of the time, Pallas kernels for 18%

profile of v2, /device:TPU:0, one launch (start us, length us, event | category | flops | bytes accessed | tf_op | source)
XLA Modules:
  0.0 390.0 jit_solution(362359398255176197)
XLA Ops:
  7.2 0.8 fusion.97
  8.1 0.2 slice_reduce_fusion.1
  8.5 1.4 convert_bitcast_fusion
  9.9 0.5 fusion.26
  10.4 0.5 fusion.20
  10.9 1.2 fusion.23
  12.1 4.3 %all-to-all-start.2 = ((s32[4,1,2048]{2,1,0:T(1,128)}), s32[4,1,2048]{2,1,0:T(1,128)S(1)}, u32[]{:S(2)}, u32[]{:S(2)}) async-start(s32[4,1,2048]{2,1,0:T(1,128)} %bitcast.22), calls=%async_computation.2 | async-start | bytes 65536 | tf_op jit(solution)/shard_map/all_to_all | solution.py:451
  16.4 0.2 fusion.66
  16.5 0.2 slice_reduce_fusion
  17.0 0.6 convert_bitcast_fusion.1
  17.6 0.5 fusion.25
  18.1 0.5 fusion.17
  18.7 1.2 fusion.24
  19.9 0.6 reshape.393.low_ref
  20.5 6.3 %all-to-all-start = ((s32[8,1,1024]{2,1,0:T(1,128)}), s32[8,1,1024]{2,1,0:T(1,128)S(1)}, u32[]{:S(2)}, u32[]{:S(2)}) async-start(s32[8,1,1024]{2,1,0:T(1,128)} %bitcast.12), calls=%async_computation | async-start | bytes 65536 | tf_op jit(solution)/shard_map/all_to_all | solution.py:445
  26.8 16.7 %select_sum.6 = bf16[2,4096,128]{2,1,0:T(8,128)(2,1)} custom-call(s32[8,512]{1,0:T(8,128)} %reshape.393.low_ref, f32[32,128]{1,0:T(8,128)} %get-tuple-element.618.sec_ref, bf16[4096,128]{1,0:T(8,128)(2,1)} %attrs_ref.3), custom_call_target="tpu_custom_call" | custom-call | flops 8589934592 | bytes 2097152 | tf_op jit(solution)/shard_map/select_sum/pallas_call | solution.py:64
  43.5 3.6 all-to-all-start.3
  47.1 0.6 reshape.386.low_ref
  47.7 16.7 %select_sum.4 = bf16[2,4096,128]{2,1,0:T(8,128)(2,1)} custom-call(s32[8,512]{1,0:T(8,128)} %reshape.386.low_ref, f32[32,128]{1,0:T(8,128)} %get-tuple-element.620.sec_ref, bf16[4096,128]{1,0:T(8,128)(2,1)} %attrs_ref.2), custom_call_target="tpu_custom_call" | custom-call | flops 8589934592 | bytes 2097152 | tf_op jit(solution)/shard_map/select_sum/pallas_call | solution.py:64
  64.4 8.3 %all-to-all-done.3 = bf16[4,2048,128]{2,1,0:T(8,128)(2,1)S(1)} async-done(((bf16[4,2048,128]{2,1,0:T(8,128)(2,1)}), bf16[4,2048,128]{2,1,0:T(8,128)(2,1)S(1)}, u32[]{:S(2)}, u32[]{:S(2)}) %all-to-all-start.3) | async-done | bytes 2097184 | tf_op jit(solution)/shard_map/all_to_all | solution.py:450
  72.8 1.3 copy-done.5
  74.1 6.0 %all-to-all-start.1 = ((bf16[8,1024,128]{2,1,0:T(8,128)(2,1)}), bf16[8,1024,128]{2,1,0:T(8,128)(2,1)S(1)}, u32[]{:S(2)}, u32[]{:S(2)}) async-start(bf16[8,1024,128]{2,1,0:T(8,128)(2,1)} %bitcast.107), calls=%async_computation.1 | async-start | bytes 4194304 | tf_op jit(solution)/shard_map/all_to_all | solution.py:444
  80.2 0.6 fusion.81.sec_ref
  80.8 0.6 fusion.79.low_ref
  81.5 0.9 fusion.8
  82.4 18.6 %select_sum.7 = f32[2,2048,128]{2,1,0:T(8,128)} custom-call(s32[16,512]{1,0:T(8,128)} %fusion.79.low_ref, f32[64,128]{1,0:T(8,128)} %fusion.81.sec_ref, bf16[8192,128]{1,0:T(8,128)(2,1)} %bitcast.109), custom_call_target="tpu_custom_call" | custom-call | flops 8589934592 | bytes 4194304 | tf_op jit(solution)/shard_map/select_sum/pallas_call | solution.py:64
  101.0 3.1 pad_maximum_fusion.1
  104.1 0.2 all-reduce.3.cloned.1.call-start
  104.3 0.6 fusion.76.sec_ref
  105.0 0.6 fusion.74.low_ref
  105.7 0.9 fusion.7
  106.6 44.1 %all-to-all-done.1 = bf16[8,1024,128]{2,1,0:T(8,128)(2,1)S(1)} async-done(((bf16[8,1024,128]{2,1,0:T(8,128)(2,1)}), bf16[8,1024,128]{2,1,0:T(8,128)(2,1)S(1)}, u32[]{:S(2)}, u32[]{:S(2)}) %all-to-all-start.1) | async-done | bytes 2097184 | tf_op jit(solution)/shard_map/all_to_all | solution.py:444
  150.7 1.3 copy-done.4
  152.0 18.6 %select_sum.5 = f32[2,2048,128]{2,1,0:T(8,128)} custom-call(s32[16,512]{1,0:T(8,128)} %fusion.74.low_ref, f32[64,128]{1,0:T(8,128)} %fusion.76.sec_ref, bf16[8192,128]{1,0:T(8,128)(2,1)} %bitcast.108), custom_call_target="tpu_custom_call" | custom-call | flops 8589934592 | bytes 4194304 | tf_op jit(solution)/shard_map/select_sum/pallas_call | solution.py:64
  170.6 3.1 pad_maximum_fusion
  173.7 47.7 %all-reduce.5.cloned.1.call-done = f32[4128,128]{1,0:T(8,128)} async-done(((f32[4128,128]{1,0:T(8,128)}), f32[4128,128]{1,0:T(8,128)}) %all-reduce.5.cloned.1.call-update) | async-done | bytes 2113552 | tf_op jit(solution)/shard_map/psum | solution.py:136
  221.4 1.3 add_bitcast_fusion
  222.7 2.9 fusion.121
  225.6 1.3 copy.16.firm_ref
  227.0 48.0 %all-reduce.3.cloned.1.call-done = f32[4128,128]{1,0:T(8,128)} async-done(((f32[4128,128]{1,0:T(8,128)}), f32[4128,128]{1,0:T(8,128)}) %all-reduce.3.cloned.1.call-update) | async-done | bytes 2113552 | tf_op jit(solution)/shard_map/psum | solution.py:136
  274.9 1.3 add_bitcast_fusion.1
  276.3 1.9 slice_divide_fusion.1
  278.2 0.4 convolution_convert_fusion.proj_ref
  278.7 0.9 copy-done.3
  279.5 101.2 %sweeps.1 = (f32[32,128]{1,0:T(8,128)S(1)}, f32[32,128]{1,0:T(8,128)S(1)}, f32[8,128]{1,0:T(8,128)}) custom-call(bf16[4096,128]{1,0:T(8,128)(2,1)S(1)} %convolution_convert_fusion.proj_ref, bf16[128,4096]{1,0:T(8,128)(2,1)} %copy.16.firm_ref, f32[32,128]{1,0:T(8,128)} %get-tuple-element.636.wmass_ref, f32[32,128]{1,0:T(8,128)} %get-tuple-element.633.fmass_ref), custom_call_target="tpu_custom_call" | custom-call | tf_op jit(solution)/shard_map/sweeps/pallas_call | solution.py:395
  380.7 1.2 slice.63
  382.6 0.6 conditional.1
  382.6 0.6 bitcast_subtract_fusion
  (31 shorter events, 1.0 us)
Async XLA Ops:
  7.2 271.1 %copy-start = (bf16[128,128]{1,0:T(8,128)(2,1)S(1)}, bf16[128,128]{1,0:T(8,128)(2,1)}, u32[]{:S(2)}) copy-start(bf16[128,128]{1,0:T(8,128)(2,1)} %param.21) | copy-start | bytes 98308
  9.8 6.5 %copy-start.6 = (s32[4096]{0:T(1024)S(1)}, s32[4096]{0:T(1024)}, u32[]{:S(2)}) copy-start(s32[4096]{0:T(1024)} %param.17) | copy-start | bytes 49156
  12.1 8.4 %all-to-all-start.2 = ((s32[4,1,2048]{2,1,0:T(1,128)}), s32[4,1,2048]{2,1,0:T(1,128)S(1)}, u32[]{:S(2)}, u32[]{:S(2)}) async-start(s32[4,1,2048]{2,1,0:T(1,128)} %bitcast.22), calls=%async_computation.2 | async-start | bytes 65536 | tf_op jit(solution)/shard_map/all_to_all | solution.py:451
  20.5 23.0 %all-to-all-start = ((s32[8,1,1024]{2,1,0:T(1,128)}), s32[8,1,1024]{2,1,0:T(1,128)S(1)}, u32[]{:S(2)}, u32[]{:S(2)}) async-start(s32[8,1,1024]{2,1,0:T(1,128)} %bitcast.12), calls=%async_computation | async-start | bytes 65536 | tf_op jit(solution)/shard_map/all_to_all | solution.py:445
  43.5 29.3 %all-to-all-start.3 = ((bf16[4,2048,128]{2,1,0:T(8,128)(2,1)}), bf16[4,2048,128]{2,1,0:T(8,128)(2,1)S(1)}, u32[]{:S(2)}, u32[]{:S(2)}) async-start(bf16[4,2048,128]{2,1,0:T(8,128)(2,1)} %bitcast.110), calls=%async_computation.3 | async-start | bytes 4194304 | tf_op jit(solution)/shard_map/all_to_all | solution.py:450
  72.8 1.3 copy-start.5
  74.1 76.6 %all-to-all-start.1 = ((bf16[8,1024,128]{2,1,0:T(8,128)(2,1)}), bf16[8,1024,128]{2,1,0:T(8,128)(2,1)S(1)}, u32[]{:S(2)}, u32[]{:S(2)}) async-start(bf16[8,1024,128]{2,1,0:T(8,128)(2,1)} %bitcast.107), calls=%async_computation.1 | async-start | bytes 4194304 | tf_op jit(solution)/shard_map/all_to_all | solution.py:444
  80.0 141.3 %all-reduce.5.cloned.1.call-start = ((), (), s32[]{:S(2)}) async-start(), calls=%async_computation.5 | async-start | bytes 4227072 | tf_op jit(solution)/shard_map/psum | solution.py:136
  104.1 170.8 %all-reduce.3.cloned.1.call-start = ((), (), s32[]{:S(2)}) async-start(), calls=%async_computation.4 | async-start | bytes 4227072 | tf_op jit(solution)/shard_map/psum | solution.py:136
  150.7 1.3 copy-start.4
  225.6 52.6 %copy-start.1 = (bf16[4096,128]{1,0:T(8,128)(2,1)}, bf16[4096,128]{1,0:T(8,128)(2,1)S(1)}, u32[]{:S(2)}) copy-start(bf16[4096,128]{1,0:T(8,128)(2,1)S(1)} %get-tuple-element.616) | copy-start | bytes 3145732
  278.2 1.3 copy-start.3
  279.5 103.0 %copy-start.2 = (bf16[4096,128]{1,0:T(8,128)(2,1)}, bf16[4096,128]{1,0:T(8,128)(2,1)S(1)}, u32[]{:S(2)}) copy-start(bf16[4096,128]{1,0:T(8,128)(2,1)S(1)} %convolution_convert_fusion.proj_ref) | copy-start | bytes 3145732
Sparse Core Ops, SparseCore 0:
  104.2 117.1 all-reduce.4
  223.8 51.1 all-reduce.2

commit v3 on v2

--- a/solution.py
+++ b/solution.py
@@ -16,7 +16,7 @@
 MESH = pl.DeviceIdType.MESH
 
 
-def select_kernel(chunk, wide, low_ref, sec_ref, attrs_ref, out_ref, rhs_ref):
+def select_kernel(chunk, wide, used_ref, low_ref, sec_ref, attrs_ref, after_ref, out_ref, rhs_ref, sum_ref):
     rows, width = attrs_ref.shape
     block = out_ref.shape[1]
     step = pl.program_id(0)
@@ -41,22 +41,27 @@
         lax.fori_loop(0, rows // LANES, fill, 0)
 
     target = lax.broadcasted_iota(jnp.int32, (block, chunk), 0) + step * block
-    total = jnp.zeros((block, wide * width), jnp.float32)
+    sum_ref[...] = jnp.zeros_like(sum_ref)
     for c in range(rows // chunk):
-        hit = jnp.where(low_ref[c : c + 1, :] == target, 1.0, 0.0).astype(jnp.bfloat16)
-        total = total + jnp.dot(
-            hit, rhs_ref[c * chunk : (c + 1) * chunk, :], preferred_element_type=jnp.float32
-        )
+
+        @pl.when(used_ref[c] > 0)
+        def _(c=c):
+            hit = jnp.where(low_ref[c : c + 1, :] == target, 1.0, 0.0).astype(jnp.bfloat16)
+            sum_ref[...] += jnp.dot(
+                hit, rhs_ref[c * chunk : (c + 1) * chunk, :], preferred_element_type=jnp.float32
+            )
+
     for s in range(wide):
-        out_ref[s] = total[:, s * width : (s + 1) * width].astype(out_ref.dtype)
-
-
-def select_sum(ids, attrs, count, dtype):
+        out_ref[s] = sum_ref[:, s * width : (s + 1) * width].astype(out_ref.dtype)
+
+
+def select_sum(ids, attrs, count, dtype, after):
     rows, width = attrs.shape
     wide = 2
     span = count // wide
     block = math.gcd(span, 256)
     chunk = math.gcd(rows, 512)
+    used = jnp.any(ids.reshape(rows // chunk, chunk) < count, axis=1).astype(jnp.int32)
     sec = ids // span
     low = (ids - sec * span).reshape(rows // chunk, chunk)
     sec = sec.astype(jnp.float32).reshape(rows // LANES, LANES)
@@ -65,19 +70,28 @@
         functools.partial(select_kernel, chunk, wide),
         grid=(span // block,),
         out_shape=jax.ShapeDtypeStruct((wide, span, width), dtype),
-        in_specs=[whole(low.shape), whole(sec.shape), whole(attrs.shape)],
+        in_specs=[
+            pl.BlockSpec(memory_space=pltpu.SMEM),
+            whole(low.shape),
+            whole(sec.shape),
+            whole(attrs.shape),
+            pl.BlockSpec(memory_space=pl.ANY),
+        ],
         out_specs=pl.BlockSpec((wide, block, width), lambda i: (0, i, 0)),
-        scratch_shapes=[pltpu.VMEM((rows, wide * width), jnp.bfloat16)],
+        scratch_shapes=[
+            pltpu.VMEM((rows, wide * width), jnp.bfloat16),
+            pltpu.VMEM((block, wide * width), jnp.float32),
+        ],
         compiler_params=pltpu.CompilerParams(vmem_limit_bytes=VMEM_BYTES),
         cost_estimate=pl.CostEstimate(
             flops=2 * rows * count * width, bytes_accessed=rows * width * 4, transcendentals=0
         ),
         name="select_sum",
-    )(low, sec, attrs)
+    )(used, low, sec, attrs, after)
     return out.reshape(count, width)
 
 
-def pack_records(type_ids, attrs, tile, groups, capacity):
+def pack_records(type_ids, attrs, tile, groups, capacity, after):
     rows = type_ids.shape[0]
     owner = type_ids // tile
     local = type_ids - owner * tile
@@ -93,12 +107,15 @@
     )
     rank = jnp.sum(jnp.where(hits, within - 1.0 + before[:, :, None], 0.0), axis=0)
     place = (grid * capacity + rank.astype(jnp.int32)).reshape(rows)
-    sent_attrs = select_sum(place, attrs, groups * capacity, jnp.bfloat16)
+    sent_attrs = select_sum(place, attrs, groups * capacity, jnp.bfloat16, after)
     high, lowd = local // 64, local % 64
-    filled = jnp.full((groups * capacity,), tile, jnp.int32)
     chosen = place_ids(place, jnp.stack([high, lowd, jnp.ones_like(high)]), groups, capacity)
-    sent_ids = jnp.where(chosen[2] > 0.5, (chosen[0] * 64.0 + chosen[1]).astype(jnp.int32), filled)
-    return (sent_attrs.reshape(groups, capacity, attrs.shape[1]), sent_ids.reshape(groups, capacity))
+    chosen = chosen.reshape(3, groups, capacity // LANES, LANES)
+    high = jnp.where(chosen[2] > 0.5, chosen[0], float(tile // 64))
+    sent_attrs = sent_attrs.reshape(groups, capacity, attrs.shape[1])
+    return jnp.concatenate(
+        [sent_attrs, high.astype(jnp.bfloat16), chosen[1].astype(jnp.bfloat16)], axis=1
+    )
 
 
 def place_ids(place, digits, groups, capacity):
@@ -115,10 +132,10 @@
     return jnp.stack(out).reshape(digits.shape[0], slots)
 
 
-def pool_records(recv_attrs, recv_ids, tile):
+def pool_records(recv_attrs, recv_ids, tile, after):
     width = recv_attrs.shape[2]
     flat_ids = recv_ids.reshape(-1)
-    totals = select_sum(flat_ids, recv_attrs.reshape(-1, width), tile, jnp.float32)
+    totals = select_sum(flat_ids, recv_attrs.reshape(-1, width), tile, jnp.float32, after)
     high, low = flat_ids // LANES, flat_ids % LANES
     ahead = (high[None, :] == jnp.arange(tile // LANES, dtype=jnp.int32)[:, None])
     behind = (low[None, :] == jnp.arange(LANES, dtype=jnp.int32)[:, None])
@@ -128,12 +145,19 @@
         (((1,), (1,)), ((), ())),
         preferred_element_type=jnp.float32,
     )
-    return (totals, tallies.reshape(tile))
-
-
-def shared_means(sums, tally, axis):
-    tile, width = sums.shape
-    both = lax.psum(jnp.concatenate([sums, tally.reshape(tile // width, width)], axis=0), axis)
+    return jnp.concatenate([totals, tallies.reshape(tile // width, width)], axis=0)
+
+
+def moved(sent, axis, capacity):
+    got = lax.all_to_all(sent, axis, split_axis=0, concat_axis=0, tiled=True)
+    lines = capacity // LANES
+    high = got[:, capacity : capacity + lines].astype(jnp.int32)
+    low = got[:, capacity + lines :].astype(jnp.int32)
+    return (got[:, :capacity], high * 64 + low)
+
+
+def shared_means(both, tile, axis):
+    both = lax.psum(both, axis)
     tally = both[tile:].reshape(tile)
     return (both[:tile] / jnp.maximum(tally, 1.0)[:, None], tally)
 
@@ -438,20 +462,18 @@
     worker_tile = W // wa_count
     firm_tile = F // af_count
     records_all = rows * wa_count * af_count
-    sent_attrs, sent_ids = pack_records(
-        worker_ids, worker_attrs, worker_tile, wa_count, 2 * rows // wa_count
-    )
-    recv_attrs = lax.all_to_all(sent_attrs, "wa", split_axis=0, concat_axis=0, tiled=True)
-    recv_ids = lax.all_to_all(sent_ids, "wa", split_axis=0, concat_axis=0, tiled=True)
-    worker_sum, worker_tally = pool_records(recv_attrs, recv_ids, worker_tile)
-    sent_attrs, sent_ids = pack_records(
-        firm_ids, firm_attrs, firm_tile, af_count, 2 * rows // af_count
-    )
-    recv_attrs = lax.all_to_all(sent_attrs, "af", split_axis=0, concat_axis=0, tiled=True)
-    recv_ids = lax.all_to_all(sent_ids, "af", split_axis=0, concat_axis=0, tiled=True)
-    firm_sum, firm_tally = pool_records(recv_attrs, recv_ids, firm_tile)
-    worker_means, worker_tally = shared_means(worker_sum, worker_tally, "af")
-    firm_means, firm_tally = shared_means(firm_sum, firm_tally, "wa")
+    worker_sent = pack_records(
+        worker_ids, worker_attrs, worker_tile, wa_count, 2 * rows // wa_count, affinity
+    )
+    worker_got = moved(worker_sent, "wa", 2 * rows // wa_count)
+    firm_sent = pack_records(
+        firm_ids, firm_attrs, firm_tile, af_count, 2 * rows // af_count, worker_sent
+    )
+    firm_got = moved(firm_sent, "af", 2 * rows // af_count)
+    firm_both = pool_records(*firm_got, firm_tile, affinity)
+    firm_means, firm_tally = shared_means(firm_both, firm_tile, "wa")
+    worker_both = pool_records(*worker_got, worker_tile, affinity)
+    worker_means, worker_tally = shared_means(worker_both, worker_tile, "af")
     log_worker = jnp.log(worker_tally + 1.0) - jnp.log(jnp.float32(records_all + W))
     log_firm = jnp.log(firm_tally + 1.0) - jnp.log(jnp.float32(records_all + F))
     projected = jnp.dot(

time: 391 us -> 448 us (1.15)
  Pallas kernels: 172 us -> 224 us
  blocking collectives: 0 us -> 30.2 us
  waiting for transfers between devices: 148 us -> 125 us
  starting transfers between devices: 20.4 us -> 6.6 us
  other arithmetic: 20.3 us -> 30.8 us
    pallas_call x4, Pallas kernels: 70.6 us -> 123 us  [select_sum(): pl.pallas_call(functools.partial(select_kernel, chunk, wide), grid=(span...]
    all_to_all x4 -> x1, waiting for transfers between devices: 52.4 us -> 10.3 us  [moved(): got = lax.all_to_all(sent, axis, split_axis=0, concat_axis=0, tiled=True)]
    all_to_all x0 -> x1, blocking collectives: none -> 30.2 us  [moved(): got = lax.all_to_all(sent, axis, split_axis=0, concat_axis=0, tiled=True)]
    psum x2, waiting for transfers between devices: 95.7 us -> 115 us  [shared_means(): both = lax.psum(both, axis)]
    all_to_all x4 -> x1, starting transfers between devices: 20.1 us -> 6.35 us  [moved(): got = lax.all_to_all(sent, axis, split_axis=0, concat_axis=0, tiled=True)]
    concatenate x2 -> x4, other arithmetic: 6.16 us -> 10.9 us  [the longest x2 6.11 us: pool_records(): jnp.concatenate([totals, tallies.reshape(tile // width, width)], axis=0)]
    slice x0 -> x2, local copies, waits for them, and re-layouts: none -> 4.5 us  [moved(): return (got[:, :capacity], high * 64 + low)]
  transfers between devices with their start and end apart: 6 -> 3, of which waited for: 4 -> 3; matrix products, arithmetic and copies ran while one was open for 5% -> 5% of each run, Pallas kernels for 18% -> 12%
where the time goes in v3:
time: 448 us; the launch traced here: 447 us
  Pallas kernels  224 us (50%)
  waiting for transfers between devices  125 us (28%)
  other arithmetic  30.8 us (7%)
  blocking collectives  30.2 us (7%)
  between operations  14.9 us (3%)
  local copies, waits for them, and re-layouts  9.72 us (2%)
  starting transfers between devices  6.6 us (1%)
  matrix products  5.59 us (1%)
    pallas_call x4, Pallas kernels, select_sum(): pl.pallas_call(functools.partial(select_kernel, chunk, wide), grid=(span...  123 us
    psum x2, waiting for transfers between devices, shared_means(): both = lax.psum(both, axis)  115 us
    pallas_call x1, Pallas kernels, fast_sweeps(): pl.pallas_call(functools.partial(sweep_kernel, wa_size, af_size), out_sha...  101 us
    all_to_all x1, blocking collectives, moved(): got = lax.all_to_all(sent, axis, split_axis=0, concat_axis=0, tiled=True)  30.2 us
    all_to_all x1, waiting for transfers between devices, moved(): got = lax.all_to_all(sent, axis, split_axis=0, concat_axis=0, tiled=True)  10.3 us
  transfers between devices with their start and end apart: 3, of which 3 were waited for; matrix products, arithmetic and copies ran while one was open for 5% of the time, Pallas kernels for 12%

profile of v3, /device:TPU:0, one launch (start us, length us, event | category | flops | bytes accessed | tf_op | source)
XLA Modules:
  0.0 447.2 jit_solution(6710833220081785447)
XLA Ops:
  7.2 0.8 broadcast_multiply_fusion
  8.5 1.4 convert_bitcast_fusion
  9.8 0.8 broadcast_multiply_fusion.1
  11.2 1.4 convert_bitcast_fusion.1
  13.2 0.6 reshape.305.low_ref
  13.8 0.5 fusion.24
  14.3 0.5 fusion.22
  14.9 0.6 convert_element_type.127.used_ref
  15.6 0.6 reshape.298.low_ref
  16.2 0.5 fusion.23
  16.7 0.5 fusion.25
  17.2 0.5 fusion.19
  17.8 0.5 fusion.26
  18.3 35.6 %select_sum.4 = bf16[2,4096,128]{2,1,0:T(8,128)(2,1)} custom-call(s32[8]{0:T(128)} %convert_element_type.127.used_ref, s32[8,512]{1,0:T(8,128)} %reshape.298.low_ref, f32[32,128]{1,0:T(8,128)} %get-tuple-element.620.sec_ref, bf16[4096,128]{1,0:T(8,128)(2,1)} %attrs_ref.2, bf16[128,128]{1,0:T(8,128)(2,1)} %after_ref.5), custom_call_target="tpu_custom_call" | custom-call | flops 8589934592 | bytes 2097152 | tf_op jit(solution)/shard_map/select_sum/pallas_call | solution.py:69
  53.9 3.1 pad_maximum_fusion.after_ref
  57.0 35.6 %select_sum.6 = bf16[2,4096,128]{2,1,0:T(8,128)(2,1)} custom-call(s32[8]{0:T(128)} %convert_element_type.142.used_ref, s32[8,512]{1,0:T(8,128)} %reshape.305.low_ref, f32[32,128]{1,0:T(8,128)} %get-tuple-element.618.sec_ref, bf16[4096,128]{1,0:T(8,128)(2,1)} %attrs_ref.3, bf16[8,1040,128]{2,1,0:T(8,128)(2,1)} %pad_maximum_fusion.after_ref), custom_call_target="tpu_custom_call" | custom-call | flops 8589934592 | bytes 2097152 | tf_op jit(solution)/shard_map/select_sum/pallas_call | solution.py:69
  92.6 1.7 pad_maximum_fusion.1
  94.3 30.2 %all_to_all.10 = bf16[4,2080,128]{2,1,0:T(8,128)(2,1)} all-to-all(bf16[4,2080,128]{2,1,0:T(8,128)(2,1)S(1)} %pad_maximum_fusion.1), channel_id=1, replica_groups=mesh['wa'=8,'af'=4] {'af'}, dimensions={0} | all-to-all | bytes 4259840 | tf_op jit(solution)/shard_map/all_to_all | solution.py:152
  124.5 6.3 %all-to-all-start = ((bf16[8,1040,128]{2,1,0:T(8,128)(2,1)}), bf16[8,1040,128]{2,1,0:T(8,128)(2,1)S(1)}, u32[]{:S(2)}, u32[]{:S(2)}) async-start(bf16[8,1040,128]{2,1,0:T(8,128)(2,1)} %pad_maximum_fusion.after_ref), calls=%async_computation | async-start | bytes 4259840 | tf_op jit(solution)/shard_map/all_to_all | solution.py:152
  130.9 0.9 compare_reduce_fusion
  132.0 0.5 convert_element_type.153.used_ref
  132.5 0.7 convert_add_fusion
  133.3 3.0 slice.109
  136.3 0.6 fusion.81.sec_ref
  136.9 0.6 fusion.79.low_ref
  137.6 0.9 fusion.8
  138.5 27.8 %select_sum.7 = f32[2,2048,128]{2,1,0:T(8,128)} custom-call(s32[16]{0:T(128)} %convert_element_type.153.used_ref, s32[16,512]{1,0:T(8,128)} %fusion.79.low_ref, f32[64,128]{1,0:T(8,128)} %fusion.81.sec_ref, bf16[8192,128]{1,0:T(8,128)(2,1)} %bitcast.166, bf16[128,128]{1,0:T(8,128)(2,1)} %after_ref.5), custom_call_target="tpu_custom_call" | custom-call | flops 8589934592 | bytes 4194304 | tf_op jit(solution)/shard_map/select_sum/pallas_call | solution.py:69
  166.3 3.0 pad_maximum_fusion.3
  169.6 10.3 %all-to-all-done = bf16[8,1040,128]{2,1,0:T(8,128)(2,1)S(1)} async-done(((bf16[8,1040,128]{2,1,0:T(8,128)(2,1)}), bf16[8,1040,128]{2,1,0:T(8,128)(2,1)S(1)}, u32[]{:S(2)}, u32[]{:S(2)}) %all-to-all-start) | async-done | bytes 2129952 | tf_op jit(solution)/shard_map/all_to_all | solution.py:152
  179.9 0.6 fusion.76.sec_ref
  181.0 0.5 convert_element_type.138.used_ref
  181.5 1.5 slice.103
  182.9 0.6 fusion.74.low_ref
  183.6 0.9 fusion.7
  184.5 24.2 %select_sum.5 = f32[2,2048,128]{2,1,0:T(8,128)} custom-call(s32[16]{0:T(128)} %convert_element_type.138.used_ref, s32[16,512]{1,0:T(8,128)} %fusion.74.low_ref, f32[64,128]{1,0:T(8,128)} %fusion.76.sec_ref, bf16[8192,128]{1,0:T(8,128)(2,1)} %bitcast.167, bf16[128,128]{1,0:T(8,128)(2,1)} %after_ref.5), custom_call_target="tpu_custom_call" | custom-call | flops 8589934592 | bytes 4194304 | tf_op jit(solution)/shard_map/select_sum/pallas_call | solution.py:69
  208.7 3.1 pad_maximum_fusion.2
  211.8 66.7 %all-reduce.5.cloned.1.call-done = f32[4128,128]{1,0:T(8,128)} async-done(((f32[4128,128]{1,0:T(8,128)}), f32[4128,128]{1,0:T(8,128)}) %all-reduce.5.cloned.1.call-update) | async-done | bytes 2113552 | tf_op jit(solution)/shard_map/psum | solution.py:160
  278.6 1.3 add_bitcast_fusion
  279.9 2.9 fusion.126
  282.8 1.4 copy.12.firm_ref
  284.2 47.9 %all-reduce.3.cloned.1.call-done = f32[4128,128]{1,0:T(8,128)} async-done(((f32[4128,128]{1,0:T(8,128)}), f32[4128,128]{1,0:T(8,128)}) %all-reduce.3.cloned.1.call-update) | async-done | bytes 2113552 | tf_op jit(solution)/shard_map/psum | solution.py:160
  332.1 1.3 add_bitcast_fusion.1
  333.4 1.9 slice_divide_fusion.1
  335.8 0.9 copy-done.2
  336.7 101.2 %sweeps.1 = (f32[32,128]{1,0:T(8,128)S(1)}, f32[32,128]{1,0:T(8,128)S(1)}, f32[8,128]{1,0:T(8,128)}) custom-call(bf16[4096,128]{1,0:T(8,128)(2,1)S(1)} %convolution_convert_fusion.proj_ref, bf16[128,4096]{1,0:T(8,128)(2,1)} %copy.12.firm_ref, f32[32,128]{1,0:T(8,128)} %get-tuple-element.638.wmass_ref, f32[32,128]{1,0:T(8,128)} %get-tuple-element.635.fmass_ref), custom_call_target="tpu_custom_call" | custom-call | tf_op jit(solution)/shard_map/sweeps/pallas_call | solution.py:419
  437.9 1.2 slice.87
  439.8 0.6 conditional.1
  439.8 0.6 bitcast_subtract_fusion
  (42 shorter events, 3.3 us)
Async XLA Ops:
  124.5 55.4 %all-to-all-start = ((bf16[8,1040,128]{2,1,0:T(8,128)(2,1)}), bf16[8,1040,128]{2,1,0:T(8,128)(2,1)S(1)}, u32[]{:S(2)}, u32[]{:S(2)}) async-start(bf16[8,1040,128]{2,1,0:T(8,128)(2,1)} %pad_maximum_fusion.after_ref), calls=%async_computation | async-start | bytes 4259840 | tf_op jit(solution)/shard_map/all_to_all | solution.py:152
  130.8 147.7 %all-reduce.5.cloned.1.call-start = ((), (), s32[]{:S(2)}) async-start(), calls=%async_computation.3 | async-start | bytes 4227072 | tf_op jit(solution)/shard_map/psum | solution.py:160
  169.4 162.7 %all-reduce.3.cloned.1.call-start = ((), (), s32[]{:S(2)}) async-start(), calls=%async_computation.2 | async-start | bytes 4227072 | tf_op jit(solution)/shard_map/psum | solution.py:160
  282.8 52.6 %copy-start = (bf16[4096,128]{1,0:T(8,128)(2,1)}, bf16[4096,128]{1,0:T(8,128)(2,1)S(1)}, u32[]{:S(2)}) copy-start(bf16[4096,128]{1,0:T(8,128)(2,1)S(1)} %get-tuple-element.616) | copy-start | bytes 3145732
  284.2 51.2 %copy-start.3 = (bf16[128,128]{1,0:T(8,128)(2,1)S(1)}, bf16[128,128]{1,0:T(8,128)(2,1)}, u32[]{:S(2)}) copy-start(bf16[128,128]{1,0:T(8,128)(2,1)} %after_ref.5) | copy-start | bytes 98308
  335.4 1.3 copy-start.2
  336.7 103.0 %copy-start.1 = (bf16[4096,128]{1,0:T(8,128)(2,1)}, bf16[4096,128]{1,0:T(8,128)(2,1)S(1)}, u32[]{:S(2)}) copy-start(bf16[4096,128]{1,0:T(8,128)(2,1)S(1)} %convolution_convert_fusion.proj_ref) | copy-start | bytes 3145732
Sparse Core Ops, SparseCore 0:
  169.5 109.0 all-reduce.4
  280.9 51.1 all-reduce.2
